TPU v7x, 256 devices: a whole 4x4x8 slice. The times are simulated.
256 devices in a mesh: dp: 8 (over x_lo, y), member: 8 (over z), mp: 4 (over x_hi, core).
Axes of the slice: x: 4 (x_hi: 2, x_lo: 2; x = x_hi * 2 + x_lo), y: 4, z: 8, core: 2. Of those that a mesh axis runs over, the one named last changes fastest.
Arguments:
- hidden: bfloat16 [1024, 4096], P('dp', ('member', 'mp')), may hold values from -9 to 9
- w_in: bfloat16 [8, 4096, 4096], P('member', 'dp', 'mp'), may hold values from -0.09375 to 0.09375
- w_out: bfloat16 [8, 4096, 4096], P('member', 'mp', 'dp'), may hold values from -0.09375 to 0.09375
- score_vec: float32 [8, 4096], P('member'), may hold values from -1 to 1
- lengths: int32 [8, 4], P('dp'), may hold values from 1 to 64, 128 in all within a row
- reward_offset: int32 [8, 4], P('dp'), may hold values from 0 to 63
- seq_weight: float32 [8, 4], P('dp'), may hold values from -4 to 4
Outputs:
- penalized: float32 [8, 4], P('dp')
- grad_hidden: float32 [1024, 4096], P('dp', ('member', 'mp'))
- grad_in: float32 [8, 4096, 4096], P('member', 'dp', 'mp')
- grad_out: float32 [8, 4096, 4096], P('member', 'mp', 'dp')
Inputs may be any that keep to these rules, and one draw needn't show every extreme that they name: Each row of lengths sums to 128, and its largest entry is exactly 64.
All inputs are finite; a program needn't handle non-finite values.
Results may differ from a plain program's by a relative error of at most 0.018.
Values may be sent and summed in bfloat16 or wider, within the bound.
No kernel may reach another device: no remote copies, remote signals or barrier semaphores. Data moves between devices by JAX's collectives and lax.ppermute only.
A program may use at most 64 MiB of HBM per device.

v0:
```python
import jax
import jax.numpy as jnp
from jax import lax
from jax.sharding import PartitionSpec as P

PENALTY = 0.5
SPREAD_FLOOR = 0.25
EPSILON = 1e-05
PRECISE = lax.Precision.HIGHEST
AGAINST = (((1,), (1,)), ((), ()))


def joined_along(parts, dim):
    parts = jnp.moveaxis(parts, 0, dim)
    lengths = parts.shape
    return parts.reshape(*lengths[:dim], lengths[dim] * lengths[dim + 1], *lengths[dim + 2 :])


def sent_to_all(array, axis):
    devices = lax.axis_size(axis)
    return lax.all_to_all(
        jnp.broadcast_to(array[None], (devices, *array.shape)), axis, 0, 0, tiled=True
    )


def gathered_copies(array, axis, dim):
    return joined_along(sent_to_all(array, axis), dim)


def in_blocks(array, dim, devices):
    before, after = (array.shape[:dim], array.shape[dim + 1 :])
    return jnp.moveaxis(array.reshape(*before, devices, -1, *after), dim, 0)


def sum_at_owner(array, axis, dim):
    devices = lax.axis_size(axis)
    parts = lax.all_to_all(in_blocks(array, dim, devices), axis, 0, 0, tiled=True)
    return jnp.sum(parts.astype(jnp.float32), axis=0)


def of_everyone(array, axis):
    return sent_to_all(array, axis).sum(axis=0)


def in_one(arrays, axis):
    vector, at, finished = (jnp.concatenate([a.reshape(-1) for a in arrays]), 0, [])
    running = of_everyone(vector, axis)
    for a in arrays:
        finished.append(running[at : at + a.size].reshape(a.shape))
        at += a.size
    return tuple(finished)


def pooling(lengths, offsets, row_count):
    seq_ends = jnp.cumsum(lengths)
    seq_starts = seq_ends - lengths
    target = seq_starts + offsets % lengths
    places = jnp.arange(row_count, dtype=jnp.int32)[:, None]
    inside = jnp.logical_and(places >= seq_starts[None, :], places < seq_ends[None, :])
    marked = places == target[None, :]
    return inside.astype(jnp.float32) / lengths.astype(jnp.float32)[None, :] + marked.astype(
        jnp.float32
    )


def silu_slope(gate_in):
    sigmoided = jax.nn.sigmoid(gate_in)
    return sigmoided * (1.0 + gate_in * (1.0 - sigmoided))


def slab_terms(left, right, slab_count):
    left_blocks = left.reshape(slab_count, left.shape[0] // slab_count, left.shape[1])
    right_blocks = right.reshape(slab_count, right.shape[0] // slab_count, right.shape[1])
    terms = jnp.einsum(
        "bsd,bsf->bdf", left_blocks, right_blocks, preferred_element_type=jnp.float32
    )
    rounded = lax.optimization_barrier(terms.astype(jnp.bfloat16))
    return jnp.sum(rounded.astype(jnp.float32), axis=0)


def local(hidden, w_in, w_out, score_vec, lengths, reward_offset, seq_weight):
    members = lax.axis_size("member")
    trunk_rows = lax.all_gather(hidden, ("member", "mp"), axis=1, tiled=True)
    w_first = w_in[0]
    w_second = w_out[0]
    vector = score_vec[0]
    feature_count = trunk_rows.shape[1]
    row_count = trunk_rows.shape[0]
    pooler = pooling(lengths[0], reward_offset[0], row_count)
    slab_count = lax.axis_size("dp")
    slab_cols = lax.all_to_all(trunk_rows, "dp", split_axis=1, concat_axis=0, tiled=True)
    rows_here = slab_cols
    gate_in = lax.psum_scatter(
        jnp.dot(rows_here, w_first, preferred_element_type=jnp.float32).astype(jnp.bfloat16),
        "dp",
        scatter_dimension=0,
        tiled=True,
    ).astype(jnp.float32)
    activated = jax.nn.silu(gate_in).astype(jnp.bfloat16)
    act_every = gathered_copies(activated, "dp", 0)
    branch_cols = jnp.dot(act_every, w_second, preferred_element_type=jnp.float32)
    branch = lax.all_to_all(
        branch_cols.astype(jnp.bfloat16), "dp", split_axis=0, concat_axis=1, tiled=True
    ).astype(branch_cols.dtype)
    share_sum = sum_at_owner(branch.astype(jnp.bfloat16), "mp", 1)
    col_count = share_sum.shape[1]
    col_start = lax.axis_index("mp") * col_count
    combined = (
        lax.dynamic_slice_in_dim(trunk_rows, col_start, col_count, 1).astype(jnp.float32)
        + share_sum
    )
    local_vec = lax.dynamic_slice_in_dim(vector, col_start, col_count, 0)
    squares, raw_dot = in_one(
        (jnp.sum(combined * combined, axis=1), jnp.dot(combined, local_vec, precision=PRECISE)),
        "mp",
    )
    inverse = lax.rsqrt(squares / feature_count + EPSILON)
    scores = raw_dot * inverse
    rewards = jnp.dot(scores, pooler, precision=PRECISE)
    moment_one, moment_two = in_one((rewards, rewards * rewards), "member")
    center = moment_one / members
    spread = moment_two / members - center * center
    deviation = jnp.sqrt(spread + SPREAD_FLOOR)
    penalized = center - PENALTY * deviation
    seq_pull = seq_weight[0] * (1.0 - PENALTY * (rewards - center) / deviation) / members
    tok_weight = jnp.dot(pooler, seq_pull, precision=PRECISE)
    slopes = tok_weight[:, None] * (
        local_vec[None, :] * inverse[:, None]
        - (scores * inverse * inverse / feature_count)[:, None] * combined
    )
    slope_half = slopes.astype(jnp.bfloat16)
    slope_full = gathered_copies(slope_half, "mp", 1)
    direct = lax.dynamic_update_slice_in_dim(
        jnp.zeros((slopes.shape[0], feature_count), jnp.float32), slopes, col_start, 1
    )
    slope_every = lax.all_to_all(slope_full, "dp", split_axis=1, concat_axis=0, tiled=True)
    rows_here = slope_every
    back_raw = sum_at_owner(
        lax.dot_general(rows_here, w_second, AGAINST, preferred_element_type=jnp.float32).astype(
            jnp.bfloat16
        ),
        "dp",
        0,
    )
    back_gate = (back_raw * silu_slope(gate_in)).astype(jnp.bfloat16)
    gate_every = gathered_copies(back_gate, "dp", 0)
    back_cols = lax.dot_general(gate_every, w_first, AGAINST, preferred_element_type=jnp.float32)
    hidden_term = direct + lax.all_to_all(
        back_cols.astype(jnp.bfloat16), "dp", split_axis=0, concat_axis=1, tiled=True
    ).astype(back_cols.dtype)
    grad_in = slab_terms(slab_cols, gate_every, slab_count)
    grad_out = slab_terms(act_every, slope_every, slab_count)
    grad_hidden = sum_at_owner(hidden_term.astype(jnp.bfloat16), ("member", "mp"), 1)
    return (penalized[None, :], grad_hidden, grad_in[None], grad_out[None])


def solution(mesh):
    in_specs = (
        P("dp", ("member", "mp")),
        P("member", "dp", "mp"),
        P("member", "mp", "dp"),
        P("member", None),
        P("dp", None),
        P("dp", None),
        P("dp", None),
    )
    out_specs = (
        P("dp", None),
        P("dp", ("member", "mp")),
        P("member", "dp", "mp"),
        P("member", "mp", "dp"),
    )
    return jax.shard_map(local, mesh=mesh, in_specs=in_specs, out_specs=out_specs, check_vma=False)
```

profile of v0, /device:TPU:7, one launch (start us, length us, event | category | flops | bytes accessed | tf_op | source)
XLA Modules:
  0.0 438.3 jit_solution(14327139450921481715)
XLA Ops:
  8.9 82.0 %all-gather.2.cloned.1.call-done = bf16[128,4096]{0,1:T(8,128)(2,1)} async-done(((bf16[128,128]{0,1:T(8,128)(2,1)}), bf16[128,4096]{0,1:T(8,128)(2,1)}) %all-gather.2.cloned.1.call-update) | async-done | bytes 1048592 | tf_op jit(solution)/shard_map/all_gather | solution.py:83
  92.3 18.8 %all_to_all.109 = bf16[128,8,512]{2,0,1:T(8,128)(2,1)S(1)} all-to-all(bf16[128,8,512]{2,0,1:T(8,128)(2,1)S(1)} %copy.59), channel_id=1, replica_groups=mesh['dp'=8,'member'=8,'mp'=4] {'dp'}, dimensions={1} | all-to-all | bytes 2097152 | tf_op jit(solution)/shard_map/all_to_all | solution.py:91
  111.1 2.6 convolution_convert_fusion.2
  113.7 38.4 %reduce-scatter.2.cloned.1.call-done = bf16[128,1024]{1,0:T(8,128)(2,1)} async-done(((bf16[1024,1024]{1,0:T(8,128)(2,1)}), bf16[128,1024]{1,0:T(8,128)(2,1)}) %reduce-scatter.2.cloned.1.call-update) | async-done | bytes 262160 | tf_op jit(solution)/shard_map/reduce_scatter | solution.py:93
  153.7 24.4 %all_to_all.110 = bf16[8,128,1024]{1,2,0:T(8,128)(2,1)S(1)} all-to-all(bf16[8,128,1024]{1,2,0:T(8,128)(2,1)S(1)} %broadcast_in_dim.16), channel_id=1, replica_groups=mesh['dp'=8,'member'=8,'mp'=4] {'dp'}, dimensions={0} | all-to-all | bytes 4194304 | tf_op jit(solution)/shard_map/all_to_all | solution.py:21
  178.1 2.6 copy.61
  180.7 3.8 convolution_convert_fusion.4
  184.5 2.3 copy.62
  186.8 14.2 %all_to_all.111 = bf16[8,128,512]{1,2,0:T(8,128)(2,1)} all-to-all(bf16[8,128,512]{1,2,0:T(8,128)(2,1)} %copy.62), channel_id=1, replica_groups=mesh['dp'=8,'member'=8,'mp'=4] {'dp'}, dimensions={0} | all-to-all | bytes 2097152 | tf_op jit(solution)/shard_map/all_to_all | solution.py:102
  201.0 13.3 %all-to-all-start.3 = ((bf16[4,128,1024]{1,2,0:T(8,128)(2,1)}), bf16[4,128,1024]{1,2,0:T(8,128)(2,1)}, u32[]{:S(2)}, u32[]{:S(2)}) async-start(bf16[4,128,1024]{1,2,0:T(8,128)(2,1)} %bitcast.95), calls=%async_computation.4 | async-start | bytes 2097152 | tf_op jit(solution)/shard_map/all_to_all | solution.py:37
  214.7 12.4 %all-to-all-done.3 = bf16[4,128,1024]{1,2,0:T(8,128)(2,1)} async-done(((bf16[4,128,1024]{1,2,0:T(8,128)(2,1)}), bf16[4,128,1024]{1,2,0:T(8,128)(2,1)}, u32[]{:S(2)}, u32[]{:S(2)}) %all-to-all-start.3) | async-done | bytes 1048608 | tf_op jit(solution)/shard_map/all_to_all | solution.py:37
  231.8 6.6 %all-to-all-start.4 = ((f32[4,1,256]{2,1,0:T(1,128)}), f32[4,1,256]{2,1,0:T(1,128)S(1)}, u32[]{:S(2)}, u32[]{:S(2)}) async-start(f32[4,1,256]{2,1,0:T(1,128)} %broadcast_in_dim.17), calls=%async_computation.5 | async-start | bytes 8192 | tf_op jit(solution)/shard_map/all_to_all | solution.py:21
  240.8 6.8 %all-to-all-start.5 = ((f32[8,1,8]{2,1,0:T(1,128)}), f32[8,1,8]{2,1,0:T(1,128)S(1)}, u32[]{:S(2)}, u32[]{:S(2)}) async-start(f32[8,1,8]{2,1,0:T(1,128)} %broadcast_in_dim.18), calls=%async_computation.6 | async-start | bytes 8192 | tf_op jit(solution)/shard_map/all_to_all | solution.py:21
  247.6 6.5 %all-to-all-done.5 = f32[8,1,8]{2,1,0:T(1,128)S(1)} async-done(((f32[8,1,8]{2,1,0:T(1,128)}), f32[8,1,8]{2,1,0:T(1,128)S(1)}, u32[]{:S(2)}, u32[]{:S(2)}) %all-to-all-start.5) | async-done | bytes 288 | tf_op jit(solution)/shard_map/all_to_all | solution.py:21
  255.8 20.9 %all_to_all.112 = bf16[4,128,1024]{1,2,0:T(8,128)(2,1)} all-to-all(bf16[4,128,1024]{1,2,0:T(8,128)(2,1)S(1)} %broadcast_in_dim.20), channel_id=1, replica_groups=mesh['dp'=8,'member'=8,'mp'=4] {'mp'}, dimensions={0} | all-to-all | bytes 2097152 | tf_op jit(solution)/shard_map/all_to_all | solution.py:21
  276.6 2.3 copy.65
  278.9 17.6 %all_to_all.113 = bf16[128,8,512]{2,0,1:T(8,128)(2,1)S(1)} all-to-all(bf16[128,8,512]{2,0,1:T(8,128)(2,1)} %copy.65), channel_id=1, replica_groups=mesh['dp'=8,'member'=8,'mp'=4] {'dp'}, dimensions={1} | all-to-all | bytes 2097152 | tf_op jit(solution)/shard_map/all_to_all | solution.py:136
  297.8 28.0 %all_to_all.114 = bf16[8,128,1024]{2,1,0:T(8,128)(2,1)S(1)} all-to-all(bf16[8,128,1024]{2,1,0:T(8,128)(2,1)S(1)} %bitcast.102), channel_id=1, replica_groups=mesh['dp'=8,'member'=8,'mp'=4] {'dp'}, dimensions={0} | all-to-all | bytes 4194304 | tf_op jit(solution)/shard_map/all_to_all | solution.py:37
  329.1 27.1 %all_to_all.115 = bf16[8,128,1024]{1,2,0:T(8,128)(2,1)} all-to-all(bf16[8,128,1024]{1,2,0:T(8,128)(2,1)S(1)} %broadcast_in_dim.21), channel_id=1, replica_groups=mesh['dp'=8,'member'=8,'mp'=4] {'dp'}, dimensions={0} | all-to-all | bytes 4194304 | tf_op jit(solution)/shard_map/all_to_all | solution.py:21
  356.1 3.9 copy.67
  360.1 4.1 convolution_convert_fusion.3
  364.2 5.3 %all-to-all-start.10 = ((bf16[8,128,512]{2,1,0:T(8,128)(2,1)}), bf16[8,128,512]{2,1,0:T(8,128)(2,1)}, u32[]{:S(2)}, u32[]{:S(2)}) async-start(bf16[8,128,512]{2,1,0:T(8,128)(2,1)} %bitcast.104), calls=%async_computation.11 | async-start | bytes 2097152 | tf_op jit(solution)/shard_map/all_to_all | solution.py:148
  370.1 14.2 %all-to-all-done.10 = bf16[8,128,512]{2,1,0:T(8,128)(2,1)} async-done(((bf16[8,128,512]{2,1,0:T(8,128)(2,1)}), bf16[8,128,512]{2,1,0:T(8,128)(2,1)}, u32[]{:S(2)}, u32[]{:S(2)}) %all-to-all-start.10) | async-done | bytes 1048608 | tf_op jit(solution)/shard_map/all_to_all | solution.py:148
  384.3 2.8 convert_bitcast_fusion.1
  387.1 2.9 copy.68
  390.0 2.3 add_dynamic-update-slice_fusion
  392.3 2.7 convert_element_type.95
  395.0 5.4 %all-to-all-start.11 = ((bf16[32,128,128]{1,2,0:T(8,128)(2,1)}), bf16[32,128,128]{1,2,0:T(8,128)(2,1)}, u32[]{:S(2)}, u32[]{:S(2)}) async-start(bf16[32,128,128]{1,2,0:T(8,128)(2,1)} %bitcast.94), calls=%async_computation.12 | async-start | bytes 2097152 | tf_op jit(solution)/shard_map/all_to_all | solution.py:37
  400.4 3.5 convolution_convert_fusion
  404.0 2.6 convert_reduce_fusion
  406.5 2.3 convert_bitcast_fusion
  411.9 17.5 %all-to-all-done.11 = bf16[32,128,128]{1,2,0:T(8,128)(2,1)} async-done(((bf16[32,128,128]{1,2,0:T(8,128)(2,1)}), bf16[32,128,128]{1,2,0:T(8,128)(2,1)}, u32[]{:S(2)}, u32[]{:S(2)}) %all-to-all-start.11) | async-done | bytes 1048608 | tf_op jit(solution)/shard_map/all_to_all | solution.py:37
  (61 shorter events, 24.1 us)
Async XLA Ops:
  7.2 173.5 %copy-start = (bf16[1,1024,512]{2,1,0:T(8,128)(2,1)S(1)}, bf16[1,1024,512]{2,1,0:T(8,128)(2,1)}, u32[]{:S(2)}) copy-start(bf16[1,1024,512]{2,1,0:T(8,128)(2,1)} %param.9) | copy-start | bytes 3145732
  7.2 83.7 %all-gather.2.cloned.1.call-start = ((), (), s32[]{:S(2)}) async-start(), calls=%async_computation.13 | async-start | bytes 1081344 | tf_op jit(solution)/shard_map/all_gather | solution.py:83
  8.8 143.3 %reduce-scatter.2.cloned.1.call-start = ((), (), s32[]{:S(2)}) async-start(), calls=%async_computation.14 | async-start | bytes 2359296 | tf_op jit(solution)/shard_map/reduce_scatter | solution.py:93
  92.3 18.8 %copy-start.10 = (bf16[1,512,1024]{2,1,0:T(8,128)(2,1)S(1)}, bf16[1,512,1024]{2,1,0:T(8,128)(2,1)}, u32[]{:S(2)}) copy-start(bf16[1,512,1024]{2,1,0:T(8,128)(2,1)} %param.8) | copy-start | bytes 3145732
  111.1 2.6 copy-start.3
  186.8 27.6 %copy-start.8 = (s32[1,4]{1,0:T(1,128)S(1)}, s32[1,4]{1,0:T(1,128)}, u32[]{:S(2)}) copy-start(s32[1,4]{1,0:T(1,128)} %param.11) | copy-start | bytes 52
  186.8 27.8 %copy-start.9 = (s32[1,4]{1,0:T(1,128)S(1)}, s32[1,4]{1,0:T(1,128)}, u32[]{:S(2)}) copy-start(s32[1,4]{1,0:T(1,128)} %param.12) | copy-start | bytes 52
  201.0 28.8 %copy-start.7 = (f32[1,4096]{1,0:T(1,128)S(1)}, f32[1,4096]{1,0:T(1,128)}, u32[]{:S(2)}) copy-start(f32[1,4096]{1,0:T(1,128)} %param.10) | copy-start | bytes 49156
  201.0 26.0 %all-to-all-start.3 = ((bf16[4,128,1024]{1,2,0:T(8,128)(2,1)}), bf16[4,128,1024]{1,2,0:T(8,128)(2,1)}, u32[]{:S(2)}, u32[]{:S(2)}) async-start(bf16[4,128,1024]{1,2,0:T(8,128)(2,1)} %bitcast.95), calls=%async_computation.4 | async-start | bytes 2097152 | tf_op jit(solution)/shard_map/all_to_all | solution.py:37
  214.4 39.7 %copy-start.11 = (f32[1,4]{1,0:T(1,128)S(1)}, f32[1,4]{1,0:T(1,128)}, u32[]{:S(2)}) copy-start(f32[1,4]{1,0:T(1,128)} %param.13) | copy-start | bytes 52
  228.5 1.3 copy-start.2
  231.8 8.1 %all-to-all-start.4 = ((f32[4,1,256]{2,1,0:T(1,128)}), f32[4,1,256]{2,1,0:T(1,128)S(1)}, u32[]{:S(2)}, u32[]{:S(2)}) async-start(f32[4,1,256]{2,1,0:T(1,128)} %broadcast_in_dim.17), calls=%async_computation.5 | async-start | bytes 8192 | tf_op jit(solution)/shard_map/all_to_all | solution.py:21
  240.8 13.2 %all-to-all-start.5 = ((f32[8,1,8]{2,1,0:T(1,128)}), f32[8,1,8]{2,1,0:T(1,128)S(1)}, u32[]{:S(2)}, u32[]{:S(2)}) async-start(f32[8,1,8]{2,1,0:T(1,128)} %broadcast_in_dim.18), calls=%async_computation.6 | async-start | bytes 8192 | tf_op jit(solution)/shard_map/all_to_all | solution.py:21
  296.5 1.3 copy-start.5
  325.8 1.0 copy-start.6
  364.2 20.1 %all-to-all-start.10 = ((bf16[8,128,512]{2,1,0:T(8,128)(2,1)}), bf16[8,128,512]{2,1,0:T(8,128)(2,1)}, u32[]{:S(2)}, u32[]{:S(2)}) async-start(bf16[8,128,512]{2,1,0:T(8,128)(2,1)} %bitcast.104), calls=%async_computation.11 | async-start | bytes 2097152 | tf_op jit(solution)/shard_map/all_to_all | solution.py:148
  395.0 34.4 %all-to-all-start.11 = ((bf16[32,128,128]{1,2,0:T(8,128)(2,1)}), bf16[32,128,128]{1,2,0:T(8,128)(2,1)}, u32[]{:S(2)}, u32[]{:S(2)}) async-start(bf16[32,128,128]{1,2,0:T(8,128)(2,1)} %bitcast.94), calls=%async_computation.12 | async-start | bytes 2097152 | tf_op jit(solution)/shard_map/all_to_all | solution.py:37
  404.0 2.6 copy-start.1
  404.0 2.6 copy-start.4
Sparse Core Ops, SparseCore 0:
  11.3 79.4 all-gather.1
  113.8 38.2 reduce-scatter.1
where the time goes:
time: 440 us; the launch traced here: 438 us
  waiting for transfers between devices  173 us (39%)
  blocking collectives  151 us (34%)
  starting transfers between devices  37.5 us (9%)
  local copies, waits for them, and re-layouts  23.3 us (5%)
  other arithmetic  20.4 us (5%)
  matrix products  19.4 us (4%)
  between operations  14.2 us (3%)
    all_gather x1, waiting for transfers between devices, local(): trunk_rows = lax.all_gather(hidden, ('member', 'mp'), axis=1, tiled=True)  82 us
    all_to_all x3, blocking collectives, sent_to_all(): lax.all_to_all(jnp.broadcast_to(array[None], (devices, *array.shape)), ax...  72.4 us
    reduce_scatter x1, waiting for transfers between devices, local(): lax.psum_scatter(jnp.dot(rows_here, w_first, preferred_element_type=jnp.f...  38.4 us
    all_to_all x2, waiting for transfers between devices, sum_at_owner(): lax.all_to_all(in_blocks(array, dim, devices), axis, 0, 0, tiled=True)  29.8 us
    all_to_all x1, blocking collectives, sum_at_owner(): lax.all_to_all(in_blocks(array, dim, devices), axis, 0, 0, tiled=True)  28 us
    all_to_all x2, starting transfers between devices, sum_at_owner(): lax.all_to_all(in_blocks(array, dim, devices), axis, 0, 0, tiled=True)  18.8 us
    all_to_all x1, blocking collectives, local(): lax.all_to_all(trunk_rows, 'dp', split_axis=1, concat_axis=0, tiled=True)  18.8 us
    all_to_all x1, blocking collectives, local(): lax.all_to_all(slope_full, 'dp', split_axis=1, concat_axis=0, tiled=True)  17.6 us
  transfers between devices with their start and end apart: 7, of which 7 were waited for; matrix products, arithmetic and copies ran while one was open for 3% of the time, Pallas kernels for 0%

commit v1 on v0

v1 whole, which is shorter than its diff:
```python
import itertools

import jax
import jax.numpy as jnp
from jax import lax
from jax.sharding import Mesh, PartitionSpec as P

PENALTY = 0.5
SPREAD_FLOOR = 0.25
EPSILON = 1e-05
PRECISE = lax.Precision.HIGHEST
AXES = ("xl", "y", "z", "xh", "c")
SIZES = (2, 4, 8, 2, 2)
BF16 = jnp.bfloat16
F32 = jnp.float32


def permuted(array, axes, target):
    sizes = [SIZES[AXES.index(a)] for a in axes]

    def flat(place):
        index = 0
        for i, size in zip(place, sizes):
            index = index * size + i
        return index

    pairs = [
        (flat(place), flat(target(*place))) for place in itertools.product(*map(range, sizes))
    ]
    return lax.ppermute(array, axes, pairs)


def over_xl(array):
    return permuted(array, ("xl",), lambda xl: (1 - xl,))


def over_xh(array):
    return permuted(array, ("xh",), lambda xh: (1 - xh,))


def over_diagonal(array):
    return permuted(array, ("xl", "xh"), lambda xl, xh: (1 - xl, 1 - xh))


def over_cores(array):
    return permuted(array, ("c",), lambda c: (1 - c,))


def owner_of(xl, y, z, xh, c):
    return (xl, 2 * xh + c, ((z // 4) ^ xl) * 4 + y, (z % 4) // 2, z % 2)


def to_owner(array):
    return permuted(array, AXES, owner_of)


def from_owner(array):
    places = list(itertools.product(*map(range, SIZES)))
    back = {owner_of(*place): place for place in places}
    return permuted(array, AXES, lambda *place: back[place])


def sent_to_all(array, axes):
    count = lax.axis_size(axes)
    return lax.all_to_all(
        jnp.broadcast_to(array[None], (count, *array.shape)), axes, 0, 0, tiled=True
    )


def summed_over_y(partial):
    rows = partial.shape[0] // SIZES[1]
    parts = lax.all_to_all(partial.reshape(SIZES[1], rows, -1), "y", 0, 0, tiled=True)
    return jnp.sum(parts.astype(F32), axis=0)


def gathered_over_y(array):
    return sent_to_all(array, "y").reshape(-1, array.shape[-1])


def mul(left, right):
    return jnp.dot(left, right, preferred_element_type=F32)


def mul_t(left, right):
    return lax.dot_general(left, right, (((1,), (1,)), ((), ())), preferred_element_type=F32)


def t_mul(left, right):
    return lax.dot_general(left, right, (((0,), (0,)), ((), ())), preferred_element_type=F32)


def ring_blocks(block):
    half = block.shape[0] // 2
    by_xl = over_xl(block)
    by_diagonal = over_diagonal(block)
    opposite = (over_xl(by_diagonal[:half]), over_diagonal(by_xl[half:]))
    return block, by_xl, opposite, by_diagonal


def pooling(lengths, offsets, row_count):
    seq_ends = jnp.cumsum(lengths)
    seq_starts = seq_ends - lengths
    target = seq_starts + offsets % lengths
    places = jnp.arange(row_count, dtype=jnp.int32)[:, None]
    inside = jnp.logical_and(places >= seq_starts[None, :], places < seq_ends[None, :])
    marked = places == target[None, :]
    return inside.astype(F32) / lengths.astype(F32)[None, :] + marked.astype(F32)


def silu_slope(gate_in):
    sigmoided = jax.nn.sigmoid(gate_in)
    return sigmoided * (1.0 + gate_in * (1.0 - sigmoided))


def in_three(vector):
    high = vector.astype(BF16)
    rest = vector - high.astype(F32)
    middle = rest.astype(BF16)
    low = (rest - middle.astype(F32)).astype(BF16)
    return jnp.stack([high, middle, low])


def local(hidden, w_in, w_out, score_vec, lengths, reward_offset, seq_weight):
    xl, y, z, xh, c = (lax.axis_index(a) for a in AXES)
    rows, members, features = 128, SIZES[2], 4096
    w_own, w_xl, (w_xh_a, w_xh_b), w_dg = ring_blocks(w_in[0])
    v_start, _ = lax.optimization_barrier((w_out[0], (w_xh_a, w_xh_b)))
    v_own, v_xl, (v_xh_a, v_xh_b), v_dg = ring_blocks(v_start)
    half_in, half_out = w_xh_a.shape[0], v_xh_a.shape[0]
    facts = jnp.concatenate([lengths.astype(F32), reward_offset.astype(F32), seq_weight])
    every_facts = sent_to_all(facts, "y")
    slabs = (2 * xh + c, 2 * xh + 1 - c)
    poolers, pulls = [], []
    for slab in slabs:
        mine = lax.dynamic_index_in_dim(every_facts, slab, 0, keepdims=False)
        poolers.append(pooling(mine[0].astype(jnp.int32), mine[1].astype(jnp.int32), rows))
        pulls.append(mine[2])
    pooler, weight = jnp.stack(poolers), jnp.stack(pulls)
    blocks = sent_to_all(from_owner(hidden), "z").reshape(2, 4, rows, -1)
    slab_mine = jnp.moveaxis(blocks, 1, 2).reshape(2, rows, -1)
    slab_both = jnp.concatenate([slab_mine, over_cores(slab_mine)], axis=1)
    hid_o, hid_t = slab_both[0], slab_both[1]
    part_o = (mul(hid_o, w_own) + mul(hid_t, w_xl)).astype(BF16)
    gate_o = summed_over_y(part_o)
    part_t = (
        mul(hid_o[:, :half_in], w_xh_a) + mul(hid_o[:, half_in:], w_xh_b) + mul(hid_t, w_dg)
    ).astype(BF16)
    gate_t = summed_over_y(part_t)
    gate = jnp.concatenate([gate_o, gate_t], axis=1)
    units = gate_o.shape[1]
    activated = gathered_over_y(jax.nn.silu(gate).astype(BF16))
    act_o, act_t = activated[:, :units], activated[:, units:]
    branch_o = mul(act_o, v_own) + mul(act_t[:, :half_out], v_xh_a) + mul(
        act_t[:, half_out:], v_xh_b
    )
    branch_t = mul(act_o, v_xl) + mul(act_t, v_dg)
    branch = jnp.stack([branch_o, branch_t])
    received = over_cores(branch[:, rows:].astype(BF16))
    combined = slab_mine.astype(F32) + branch[:, :rows] + received.astype(F32)
    width = combined.shape[2]
    vec = jnp.stack(
        [
            lax.dynamic_slice_in_dim(score_vec[0], (4 * xl + y) * width, width),
            lax.dynamic_slice_in_dim(score_vec[0], (4 * (1 - xl) + y) * width, width),
        ]
    )
    combined_half = combined.astype(BF16)
    combined_both = jnp.concatenate([combined_half, over_cores(combined_half)], axis=1)
    sums = jnp.stack(
        [jnp.sum(combined * combined, axis=(0, 2)), jnp.sum(combined * vec[:, None], axis=(0, 2))]
    )
    sums = jnp.stack([sums, over_cores(sums)])
    every = sent_to_all(sums.reshape(4, rows), ("y", "z")).reshape(4, members, 2, 2, rows)
    totals = jnp.sum(every, axis=0)
    inverse = lax.rsqrt(totals[:, :, 0] / features + EPSILON)
    scores = totals[:, :, 1] * inverse
    rewards = jnp.einsum("mot,ots->mos", scores, pooler, precision=PRECISE)
    center = jnp.mean(rewards, axis=0)
    spread = jnp.mean((rewards - center) ** 2, axis=0)
    deviation = jnp.sqrt(spread + SPREAD_FLOOR)
    penalized = center - PENALTY * deviation
    reward, inverse, scores = (
        lax.dynamic_index_in_dim(a, z, 0, keepdims=False) for a in (rewards, inverse, scores)
    )
    seq_pull = weight * (1.0 - PENALTY * (reward - center) / deviation) / members
    tok_weight = jnp.einsum("ots,os->ot", pooler, seq_pull, precision=PRECISE)
    by_vec = (tok_weight * inverse).reshape(-1, 1)
    by_combined = (tok_weight * scores * inverse * inverse / features).reshape(-1, 1)
    by_core = jnp.where(c == 0, penalized, penalized[::-1])
    of_row = jnp.where(y // 2 == xh, by_core, over_xh(by_core))
    reported = lax.dynamic_index_in_dim(of_row, y % 2, 0)
    com_o, com_t = combined_both[0], combined_both[1]
    thirds_o, thirds_t = in_three(vec[0]), in_three(vec[1])

    def against_out(left_o, left_t):
        own = mul_t(left_o, v_own) + mul_t(left_t, v_xl)
        other = jnp.concatenate([mul_t(left_o, v_xh_a), mul_t(left_o, v_xh_b)], axis=1) + mul_t(
            left_t, v_dg
        )
        return jnp.concatenate([own, other], axis=1)

    vec_part = jnp.sum(against_out(thirds_o, thirds_t), axis=0, keepdims=True)
    vec_out = jnp.sum(sent_to_all(vec_part, "y"), axis=0)
    com_out = summed_over_y(against_out(com_o, com_t).astype(BF16))
    piece = com_out.shape[0]
    piece_vec = lax.dynamic_slice_in_dim(by_vec, y * piece, piece, 0)
    piece_com = lax.dynamic_slice_in_dim(by_combined, y * piece, piece, 0)
    back_raw = piece_vec * vec_out - piece_com * com_out
    back_gate = gathered_over_y((back_raw * silu_slope(gate)).astype(BF16))
    back_o, back_t = back_gate[:, :units], back_gate[:, units:]
    back_w_o = mul_t(back_o, w_own) + jnp.concatenate(
        [mul_t(back_t, w_xh_a), mul_t(back_t, w_xh_b)], axis=1
    )
    back_w_t = mul_t(back_o, w_xl) + mul_t(back_t, w_dg)
    back_w = jnp.stack([back_w_o, back_w_t])
    direct = by_vec[:rows] * vec[:, None] - by_combined[:rows] * combined
    term = direct + back_w[:, :rows] + over_cores(back_w[:, rows:].astype(BF16)).astype(F32)
    pieces = jnp.moveaxis(term.astype(BF16).reshape(2, rows, 4, -1), 2, 1).reshape(8, rows, -1)
    from_heads = lax.all_to_all(pieces, "z", 0, 0, tiled=True)
    block = jnp.sum(from_heads.astype(F32), axis=0)
    grad_hidden = to_owner(block.astype(BF16)).astype(F32)
    slopes = (by_vec * vec[:, None] - by_combined * combined_both.astype(F32)).astype(BF16)

    def quarters(own, other):
        return jnp.concatenate([own, over_xl(own), over_xh(other), over_diagonal(other)])

    def feature_quarters(own, other):
        return jnp.concatenate([own, over_xl(other), over_xh(own), over_diagonal(other)])

    grad_out = t_mul(quarters(act_o, act_t), feature_quarters(slopes[0], slopes[1]))
    grad_in = t_mul(feature_quarters(hid_o, hid_t), quarters(back_o, back_t))
    return (reported, grad_hidden, grad_in[None], grad_out[None])


def solution(mesh):
    fine = Mesh(mesh.devices.reshape(SIZES), AXES)
    dp, member, mp = ("xl", "y"), "z", ("xh", "c")
    in_specs = (
        P(dp, (member, *mp)),
        P(member, dp, mp),
        P(member, mp, dp),
        P(member, None),
        P(dp, None),
        P(dp, None),
        P(dp, None),
    )
    out_specs = (
        P(dp, None),
        P(dp, (member, *mp)),
        P(member, dp, mp),
        P(member, mp, dp),
    )
    return jax.shard_map(local, mesh=fine, in_specs=in_specs, out_specs=out_specs, check_vma=False)
```

time: 440 us -> 264 us (0.60)
  blocking collectives: 151 us -> 0 us
  waiting for transfers between devices: 173 us -> 100 us
  starting transfers between devices: 37.5 us -> 107 us
  between operations: 14.2 us -> 1.38 us
  matrix products: 19.4 us -> 31.9 us
  other arithmetic: 20.4 us -> 8.64 us
  local copies, waits for them, and re-layouts: 23.3 us -> 13.2 us
    all_to_all x7 -> x0, blocking collectives: 151 us -> none  [the longest x3 72.4 us: sent_to_all(): lax.all_to_all(jnp.broadcast_to(array[None], (devices, *array.shape)), ax...]
    all_gather x1 -> x0, waiting for transfers between devices: 82 us -> none  [local(): trunk_rows = lax.all_gather(hidden, ('member', 'mp'), axis=1, tiled=True)]
    ppermute x0 -> x28, starting transfers between devices: none -> 62.9 us  [permuted(): return lax.ppermute(array, axes, pairs)]
    ppermute x0 -> x28, waiting for transfers between devices: none -> 58.7 us  [permuted(): return lax.ppermute(array, axes, pairs)]
    reduce_scatter x1 -> x0, waiting for transfers between devices: 38.4 us -> none  [local(): lax.psum_scatter(jnp.dot(rows_here, w_first, preferred_element_type=jnp.f...]
    all_to_all x5 -> x0, local copies, waits for them, and re-layouts: 12.5 us -> none  [the longest x2 6.49 us: sent_to_all(): lax.all_to_all(jnp.broadcast_to(array[None], (devices, *array.shape)), ax...]
    dot_general x9 -> x29, matrix products: 19.4 us -> 31.9 us  [the longest x15 13.6 us: mul_t(): lax.dot_general(left, right, (((1,), (1,)), ((), ())), preferred_element_...]
    all_to_all x5 -> x10, waiting for transfers between devices: 52.1 us -> 41.5 us  [the longest x6 21.5 us: sent_to_all(): lax.all_to_all(jnp.broadcast_to(array[None], (count, *array.shape)), axes...]
  transfers between devices with their start and end apart: 7 -> 38, of which waited for: 7 -> 16; matrix products, arithmetic and copies ran while one was open for 3% -> 20% of each run, Pallas kernels for 0% -> 0%
where the time goes in v1:
time: 264 us; the launch traced here: 262 us
  starting transfers between devices  107 us (41%)
  waiting for transfers between devices  100 us (38%)
  matrix products  31.9 us (12%)
  local copies, waits for them, and re-layouts  13.2 us (5%)
  other arithmetic  8.64 us (3%)
    ppermute x28, starting transfers between devices, permuted(): return lax.ppermute(array, axes, pairs)  62.9 us
    ppermute x28, waiting for transfers between devices, permuted(): return lax.ppermute(array, axes, pairs)  58.7 us
    all_to_all x6, starting transfers between devices, sent_to_all(): lax.all_to_all(jnp.broadcast_to(array[None], (count, *array.shape)), axes...  23.8 us
    all_to_all x6, waiting for transfers between devices, sent_to_all(): lax.all_to_all(jnp.broadcast_to(array[None], (count, *array.shape)), axes...  21.5 us
    all_to_all x3, waiting for transfers between devices, summed_over_y(): lax.all_to_all(partial.reshape(SIZES[1], rows, -1), 'y', 0, 0, tiled=True)  17.1 us
    dot_general x15, matrix products, mul_t(): lax.dot_general(left, right, (((1,), (1,)), ((), ())), preferred_element_...  13.6 us
    all_to_all x3, starting transfers between devices, summed_over_y(): lax.all_to_all(partial.reshape(SIZES[1], rows, -1), 'y', 0, 0, tiled=True)  11.4 us
    dot_general x10, matrix products, mul(): return jnp.dot(left, right, preferred_element_type=F32)  9.77 us
  transfers between devices with their start and end apart: 38, of which 16 were waited for; matrix products, arithmetic and copies ran while one was open for 20% of the time, Pallas kernels for 0%

profile of v1, /device:TPU:7, one launch (start us, length us, event | category | flops | bytes accessed | tf_op | source)
XLA Modules:
  0.0 262.1 jit_solution(17415500337745490367)
XLA Ops:
  4.1 4.2 %all-to-all-start = ((f32[4,3,4]{2,1,0:T(4,128)}), f32[4,3,4]{2,1,0:T(4,128)S(1)}, u32[]{:S(2)}, u32[]{:S(2)}) async-start(f32[4,3,4]{2,1,0:T(4,128)} %broadcast_in_dim.18), calls=%async_computation | async-start | bytes 16384 | tf_op jit(solution)/shard_map/all_to_all | solution.py:65
  8.3 11.6 %collective-permute-start = (bf16[128,128]{1,0:T(8,128)(2,1)}, bf16[128,128]{1,0:T(8,128)(2,1)S(1)}, u32[]{:S(2)}, u32[]{:S(2)}) collective-permute-start(bf16[128,128]{1,0:T(8,128)(2,1)} %param.7), channel_id=1, source_target_pairs={{0,0},{1,4},{2,8},{3,12},{4,32},{5,36},{6,40},{7,44},{8,64},{9,68}... | collective-permute-start | bytes 98312 | tf_op jit(solution)/shard_map/ppermute | solution.py:30
  20.7 5.4 %collective-permute-done = bf16[128,128]{1,0:T(8,128)(2,1)S(1)} collective-permute-done((bf16[128,128]{1,0:T(8,128)(2,1)}, bf16[128,128]{1,0:T(8,128)(2,1)S(1)}, u32[]{:S(2)}, u32[]{:S(2)}) %collective-permute-start) | collective-permute-done | bytes 32800 | tf_op jit(solution)/shard_map/ppermute | solution.py:30
  26.8 4.4 %all-to-all-start.1 = ((bf16[8,128,128]{2,1,0:T(8,128)(2,1)}), bf16[8,128,128]{2,1,0:T(8,128)(2,1)S(1)}, u32[]{:S(2)}, u32[]{:S(2)}) async-start(bf16[8,128,128]{2,1,0:T(8,128)(2,1)} %broadcast_in_dim.19), calls=%async_computation.1 | async-start | bytes 524288 | tf_op jit(solution)/shard_map/all_to_all | solution.py:65
  31.3 9.3 %all-to-all-done.1 = bf16[8,128,128]{2,1,0:T(8,128)(2,1)S(1)} async-done(((bf16[8,128,128]{2,1,0:T(8,128)(2,1)}), bf16[8,128,128]{2,1,0:T(8,128)(2,1)S(1)}, u32[]{:S(2)}, u32[]{:S(2)}) %all-to-all-start.1) | async-done | bytes 262176 | tf_op jit(solution)/shard_map/all_to_all | solution.py:65
  40.6 3.7 %collective-permute-start.1 = (bf16[2,128,512]{2,1,0:T(8,128)(2,1)S(1)}, bf16[2,128,512]{2,1,0:T(8,128)(2,1)S(1)}, u32[]{:S(2)}, u32[]{:S(2)}) collective-permute-start(bf16[2,128,512]{2,1,0:T(8,128)(2,1)S(1)} %bitcast.172), channel_id=1, source_target_pairs={{0,1},{1,0},{2,3},{3,2},{4,5},{5,4},{6,7},{7,6},{8,9},{9,8},{10,11... | collective-permute-start | bytes 786440 | tf_op jit(solution)/shard_map/ppermute | solution.py:30
  47.2 9.3 %collective-permute-start.4 = (bf16[256,1024]{1,0:T(8,128)(2,1)}, bf16[256,1024]{1,0:T(8,128)(2,1)S(1)}, u32[]{:S(2)}, u32[]{:S(2)}) collective-permute-start(bf16[256,1024]{1,0:T(8,128)(2,1)} %slice.165), channel_id=1, source_target_pairs={{0,128},{128,0},{1,129},{129,1},{2,130},{130,2},{3,131},{131,3},{4... | collective-permute-start | bytes 1572872 | tf_op jit(solution)/shard_map/ppermute | solution.py:30
  59.1 4.3 %all-to-all-start.2 = ((bf16[4,64,1024]{2,1,0:T(8,128)(2,1)}), bf16[4,64,1024]{2,1,0:T(8,128)(2,1)}, u32[]{:S(2)}, u32[]{:S(2)}) async-start(bf16[4,64,1024]{2,1,0:T(8,128)(2,1)} %bitcast.168), calls=%async_computation.2 | async-start | bytes 1048576 | tf_op jit(solution)/shard_map/all_to_all | solution.py:72
  63.9 7.9 %collective-permute-done.5 = bf16[256,1024]{1,0:T(8,128)(2,1)} collective-permute-done((bf16[256,1024]{1,0:T(8,128)(2,1)}, bf16[256,1024]{1,0:T(8,128)(2,1)}, u32[]{:S(2)}, u32[]{:S(2)}) %collective-permute-start.5) | collective-permute-done | bytes 524320 | tf_op jit(solution)/shard_map/ppermute | solution.py:30
  74.3 3.5 %all-to-all-start.3 = ((bf16[4,64,1024]{2,1,0:T(8,128)(2,1)}), bf16[4,64,1024]{2,1,0:T(8,128)(2,1)S(1)}, u32[]{:S(2)}, u32[]{:S(2)}) async-start(bf16[4,64,1024]{2,1,0:T(8,128)(2,1)} %bitcast.14), calls=%async_computation.3 | async-start | bytes 1048576 | tf_op jit(solution)/shard_map/all_to_all | solution.py:72
  79.9 5.5 %all-to-all-done.3 = bf16[4,64,1024]{2,1,0:T(8,128)(2,1)S(1)} async-done(((bf16[4,64,1024]{2,1,0:T(8,128)(2,1)}), bf16[4,64,1024]{2,1,0:T(8,128)(2,1)S(1)}, u32[]{:S(2)}, u32[]{:S(2)}) %all-to-all-start.3) | async-done | bytes 524320 | tf_op jit(solution)/shard_map/all_to_all | solution.py:72
  87.5 3.5 %all-to-all-start.4 = ((bf16[4,64,2048]{2,1,0:T(8,128)(2,1)}), bf16[4,64,2048]{2,1,0:T(8,128)(2,1)S(1)}, u32[]{:S(2)}, u32[]{:S(2)}) async-start(bf16[4,64,2048]{2,1,0:T(8,128)(2,1)} %broadcast_in_dim.20), calls=%async_computation.4 | async-start | bytes 2097152 | tf_op jit(solution)/shard_map/all_to_all | solution.py:65
  91.5 10.0 %collective-permute-done.8 = bf16[1024,512]{1,0:T(8,128)(2,1)S(1)} collective-permute-done((bf16[1024,512]{1,0:T(8,128)(2,1)}, bf16[1024,512]{1,0:T(8,128)(2,1)S(1)}, u32[]{:S(2)}, u32[]{:S(2)}) %collective-permute-start.8) | collective-permute-done | bytes 1048608 | tf_op jit(solution)/shard_map/ppermute | solution.py:30
  108.5 11.2 %collective-permute-done.9 = bf16[512,512]{1,0:T(8,128)(2,1)} collective-permute-done((bf16[512,512]{1,0:T(8,128)(2,1)}, bf16[512,512]{1,0:T(8,128)(2,1)}, u32[]{:S(2)}, u32[]{:S(2)}) %collective-permute-start.9) | collective-permute-done | bytes 524320 | tf_op jit(solution)/shard_map/ppermute | solution.py:30
  131.4 4.4 %all-to-all-start.6 = ((f32[4,1,2048]{2,1,0:T(1,128)}), f32[4,1,2048]{2,1,0:T(1,128)S(1)}, u32[]{:S(2)}, u32[]{:S(2)}) async-start(f32[4,1,2048]{2,1,0:T(1,128)} %broadcast_in_dim.23), calls=%async_computation.6 | async-start | bytes 65536 | tf_op jit(solution)/shard_map/all_to_all | solution.py:65
  135.8 4.3 %all-to-all-done.6 = f32[4,1,2048]{2,1,0:T(1,128)S(1)} async-done(((f32[4,1,2048]{2,1,0:T(1,128)}), f32[4,1,2048]{2,1,0:T(1,128)S(1)}, u32[]{:S(2)}, u32[]{:S(2)}) %all-to-all-start.6) | async-done | bytes 32800 | tf_op jit(solution)/shard_map/all_to_all | solution.py:65
  140.7 3.9 %all-to-all-start.5 = ((f32[32,4,128]{2,1,0:T(4,128)}), f32[32,4,128]{2,1,0:T(4,128)S(1)}, u32[]{:S(2)}, u32[]{:S(2)}) async-start(f32[32,4,128]{2,1,0:T(4,128)} %broadcast_in_dim.22), calls=%async_computation.5 | async-start | bytes 131072 | tf_op jit(solution)/shard_map/all_to_all | solution.py:65
  146.2 2.7 %collective-permute-start.22 = (bf16[256,1024]{1,0:T(8,128)(2,1)}, bf16[256,1024]{1,0:T(8,128)(2,1)}, u32[]{:S(2)}, u32[]{:S(2)}) collective-permute-start(bf16[256,1024]{1,0:T(8,128)(2,1)} %get-tuple-element.18), channel_id=1, source_target_pairs={{0,128},{128,0},{1,129},{129,1},{2,130},{130,2},{3,131},{131,3},{4... | collective-permute-start | bytes 1572872 | tf_op jit(solution)/shard_map/ppermute | solution.py:30
  149.0 2.8 %collective-permute-start.13 = (bf16[2,128,512]{2,1,0:T(8,128)(2,1)S(1)}, bf16[2,128,512]{2,1,0:T(8,128)(2,1)S(1)}, u32[]{:S(2)}, u32[]{:S(2)}) collective-permute-start(bf16[2,128,512]{2,1,0:T(8,128)(2,1)S(1)} %get-tuple-element.12), channel_id=1, source_target_pairs={{0,1},{1,0},{2,3},{3,2},{4,5},{5,4},{6,7},{7,6},{8,9},{9,8},{10,11... | collective-permute-start | bytes 786440 | tf_op jit(solution)/shard_map/ppermute | solution.py:30
  160.9 3.6 %all-to-all-start.7 = ((bf16[4,64,2048]{2,1,0:T(8,128)(2,1)}), bf16[4,64,2048]{2,1,0:T(8,128)(2,1)S(1)}, u32[]{:S(2)}, u32[]{:S(2)}) async-start(bf16[4,64,2048]{2,1,0:T(8,128)(2,1)} %pad_maximum_fusion), calls=%async_computation.7 | async-start | bytes 2097152 | tf_op jit(solution)/shard_map/all_to_all | solution.py:72
  164.7 11.6 %all-to-all-done.7 = bf16[4,64,2048]{2,1,0:T(8,128)(2,1)S(1)} async-done(((bf16[4,64,2048]{2,1,0:T(8,128)(2,1)}), bf16[4,64,2048]{2,1,0:T(8,128)(2,1)S(1)}, u32[]{:S(2)}, u32[]{:S(2)}) %all-to-all-start.7) | async-done | bytes 1048608 | tf_op jit(solution)/shard_map/all_to_all | solution.py:72
  177.8 3.5 %all-to-all-start.8 = ((bf16[4,64,2048]{2,1,0:T(8,128)(2,1)}), bf16[4,64,2048]{2,1,0:T(8,128)(2,1)S(1)}, u32[]{:S(2)}, u32[]{:S(2)}) async-start(bf16[4,64,2048]{2,1,0:T(8,128)(2,1)} %broadcast_in_dim.24), calls=%async_computation.8 | async-start | bytes 2097152 | tf_op jit(solution)/shard_map/all_to_all | solution.py:65
  185.7 6.3 %all-to-all-done.8 = bf16[4,64,2048]{2,1,0:T(8,128)(2,1)S(1)} async-done(((bf16[4,64,2048]{2,1,0:T(8,128)(2,1)}), bf16[4,64,2048]{2,1,0:T(8,128)(2,1)S(1)}, u32[]{:S(2)}, u32[]{:S(2)}) %all-to-all-start.8) | async-done | bytes 1048608 | tf_op jit(solution)/shard_map/all_to_all | solution.py:65
  195.6 5.5 %collective-permute-start.14 = (bf16[2,128,512]{2,1,0:T(8,128)(2,1)S(1)}, bf16[2,128,512]{2,1,0:T(8,128)(2,1)S(1)}, u32[]{:S(2)}, u32[]{:S(2)}) collective-permute-start(bf16[2,128,512]{2,1,0:T(8,128)(2,1)S(1)} %fusion.52), channel_id=1, source_target_pairs={{0,1},{1,0},{2,3},{3,2},{4,5},{5,4},{6,7},{7,6},{8,9},{9,8},{10,11... | collective-permute-start | bytes 786440 | tf_op jit(solution)/shard_map/ppermute | solution.py:30
  203.5 3.0 %collective-permute-start.26 = (bf16[256,512]{1,0:T(8,128)(2,1)S(1)}, bf16[256,512]{1,0:T(8,128)(2,1)}, u32[]{:S(2)}, u32[]{:S(2)}) collective-permute-start(bf16[256,512]{1,0:T(8,128)(2,1)S(1)} %get-tuple-element.22), channel_id=1, source_target_pairs={{0,2},{2,0},{1,3},{3,1},{4,6},{6,4},{5,7},{7,5},{8,10},{10,8},{9,1... | collective-permute-start | bytes 786440 | tf_op jit(solution)/shard_map/ppermute | solution.py:30
  208.0 3.0 %collective-permute-done.27 = bf16[256,512]{1,0:T(8,128)(2,1)S(1)} collective-permute-done((bf16[256,512]{1,0:T(8,128)(2,1)S(1)}, bf16[256,512]{1,0:T(8,128)(2,1)S(1)}, u32[]{:S(2)}, u32[]{:S(2)}) %collective-permute-start.27) | collective-permute-done | bytes 262176 | tf_op jit(solution)/shard_map/ppermute | solution.py:30
  211.7 8.6 %all-to-all-start.9 = ((bf16[8,128,128]{2,1,0:T(8,128)(2,1)}), bf16[8,128,128]{2,1,0:T(8,128)(2,1)S(1)}, u32[]{:S(2)}, u32[]{:S(2)}) async-start(bf16[8,128,128]{2,1,0:T(8,128)(2,1)} %bitcast.48), calls=%async_computation.9 | async-start | bytes 524288 | tf_op jit(solution)/shard_map/all_to_all | solution.py:219
  222.6 4.3 %fusion.16 = f32[1,1024,512]{2,1,0:T(8,128)} fusion(bf16[256,1024]{1,0:T(8,128)(2,1)} %collective-permute-done.24, bf16[256,1024]{1,0:T(8,128)(2,1)} %collective-permute-done.23, bf16[256,1024]{1,0:T(8,128)(2,1)} %collective-permute-done.22, bf16[256,1024]{1,0:T(8,128)(2,1)} %get-tuple-element.18, bf16[256,512]{1,0:T(8,128)(2,1)S(1)} %collective-permute-done.27, ...), kind=kOutput, calls=%fused_computation.17 | convolution fusion | flops 1086324736 | bytes 5242880 | tf_op jit(solution)/shard_map/dot_general | solution.py:89
  226.8 2.9 %all-to-all-done.9 = bf16[8,128,128]{2,1,0:T(8,128)(2,1)S(1)} async-done(((bf16[8,128,128]{2,1,0:T(8,128)(2,1)}), bf16[8,128,128]{2,1,0:T(8,128)(2,1)S(1)}, u32[]{:S(2)}, u32[]{:S(2)}) %all-to-all-start.9) | async-done | bytes 262176 | tf_op jit(solution)/shard_map/all_to_all | solution.py:219
  229.7 16.3 %collective-permute-done.17 = bf16[256,512]{1,0:T(8,128)(2,1)} collective-permute-done((bf16[256,512]{1,0:T(8,128)(2,1)S(1)}, bf16[256,512]{1,0:T(8,128)(2,1)}, u32[]{:S(2)}, u32[]{:S(2)}) %collective-permute-start.17) | collective-permute-done | bytes 262176 | tf_op jit(solution)/shard_map/ppermute | solution.py:30
  246.0 11.4 %collective-permute-start.15 = (bf16[128,128]{1,0:T(8,128)(2,1)S(1)}, bf16[128,128]{1,0:T(8,128)(2,1)S(1)}, u32[]{:S(2)}, u32[]{:S(2)}) collective-permute-start(bf16[128,128]{1,0:T(8,128)(2,1)S(1)} %reduce_sum.112), channel_id=1, source_target_pairs={{0,0},{1,32},{2,64},{3,96},{4,1},{5,33},{6,65},{7,97},{8,2},{9,34}... | collective-permute-start | bytes 98312 | tf_op jit(solution)/shard_map/ppermute | solution.py:30
  257.5 4.0 %fusion.19 = f32[1,512,1024]{2,1,0:T(8,128)} fusion(bf16[256,1024]{1,0:T(8,128)(2,1)S(1)} %collective-permute-done.21, bf16[256,1024]{1,0:T(8,128)(2,1)} %collective-permute-done.20, bf16[256,1024]{1,0:T(8,128)(2,1)} %collective-permute-done.19, bf16[256,1024]{1,0:T(8,128)(2,1)S(1)} %get-tuple-element.20, bf16[256,512]{1,0:T(8,128)(2,1)} %collective-permute-done.18, ...), kind=kOutput, calls=%fused_computation.18 | convolution fusion | flops 1086324736 | bytes 5242880 | tf_op jit(solution)/shard_map/dot_general | solution.py:89
  (184 shorter events, 64.9 us)
Async XLA Ops:
  0.6 45.8 %collective-permute-start.3 = (bf16[512,1024]{1,0:T(8,128)(2,1)}, bf16[512,1024]{1,0:T(8,128)(2,1)S(1)}, u32[]{:S(2)}, u32[]{:S(2)}) collective-permute-start(bf16[512,1024]{1,0:T(8,128)(2,1)} %bitcast.166), channel_id=1, source_target_pairs={{0,130},{2,128},{128,2},{130,0},{1,131},{3,129},{129,3},{131,1},{4... | collective-permute-start | bytes 3145736 | tf_op jit(solution)/shard_map/ppermute | solution.py:30
  0.7 55.8 %collective-permute-start.2 = (bf16[512,1024]{1,0:T(8,128)(2,1)}, bf16[512,1024]{1,0:T(8,128)(2,1)S(1)}, u32[]{:S(2)}, u32[]{:S(2)}) collective-permute-start(bf16[512,1024]{1,0:T(8,128)(2,1)} %bitcast.167), channel_id=1, source_target_pairs={{0,128},{128,0},{1,129},{129,1},{2,130},{130,2},{3,131},{131,3},{4... | collective-permute-start | bytes 3145736 | tf_op jit(solution)/shard_map/ppermute | solution.py:30
  4.1 16.6 %all-to-all-start = ((f32[4,3,4]{2,1,0:T(4,128)}), f32[4,3,4]{2,1,0:T(4,128)S(1)}, u32[]{:S(2)}, u32[]{:S(2)}) async-start(f32[4,3,4]{2,1,0:T(4,128)} %broadcast_in_dim.18), calls=%async_computation | async-start | bytes 16384 | tf_op jit(solution)/shard_map/all_to_all | solution.py:65
  8.3 17.7 %collective-permute-start = (bf16[128,128]{1,0:T(8,128)(2,1)}, bf16[128,128]{1,0:T(8,128)(2,1)S(1)}, u32[]{:S(2)}, u32[]{:S(2)}) collective-permute-start(bf16[128,128]{1,0:T(8,128)(2,1)} %param.7), channel_id=1, source_target_pairs={{0,0},{1,4},{2,8},{3,12},{4,32},{5,36},{6,40},{7,44},{8,64},{9,68}... | collective-permute-start | bytes 98312 | tf_op jit(solution)/shard_map/ppermute | solution.py:30
  26.8 13.8 %all-to-all-start.1 = ((bf16[8,128,128]{2,1,0:T(8,128)(2,1)}), bf16[8,128,128]{2,1,0:T(8,128)(2,1)S(1)}, u32[]{:S(2)}, u32[]{:S(2)}) async-start(bf16[8,128,128]{2,1,0:T(8,128)(2,1)} %broadcast_in_dim.19), calls=%async_computation.1 | async-start | bytes 524288 | tf_op jit(solution)/shard_map/all_to_all | solution.py:65
  47.2 25.9 %collective-permute-start.4 = (bf16[256,1024]{1,0:T(8,128)(2,1)}, bf16[256,1024]{1,0:T(8,128)(2,1)S(1)}, u32[]{:S(2)}, u32[]{:S(2)}) collective-permute-start(bf16[256,1024]{1,0:T(8,128)(2,1)} %slice.165), channel_id=1, source_target_pairs={{0,128},{128,0},{1,129},{129,1},{2,130},{130,2},{3,131},{131,3},{4... | collective-permute-start | bytes 1572872 | tf_op jit(solution)/shard_map/ppermute | solution.py:30
  57.4 14.4 %collective-permute-start.5 = (bf16[256,1024]{1,0:T(8,128)(2,1)}, bf16[256,1024]{1,0:T(8,128)(2,1)}, u32[]{:S(2)}, u32[]{:S(2)}) collective-permute-start(bf16[256,1024]{1,0:T(8,128)(2,1)} %slice.167), channel_id=1, source_target_pairs={{0,130},{2,128},{128,2},{130,0},{1,131},{3,129},{129,3},{131,1},{4... | collective-permute-start | bytes 1572872 | tf_op jit(solution)/shard_map/ppermute | solution.py:30
  59.1 15.1 %all-to-all-start.2 = ((bf16[4,64,1024]{2,1,0:T(8,128)(2,1)}), bf16[4,64,1024]{2,1,0:T(8,128)(2,1)}, u32[]{:S(2)}, u32[]{:S(2)}) async-start(bf16[4,64,1024]{2,1,0:T(8,128)(2,1)} %bitcast.168), calls=%async_computation.2 | async-start | bytes 1048576 | tf_op jit(solution)/shard_map/all_to_all | solution.py:72
  74.3 11.2 %all-to-all-start.3 = ((bf16[4,64,1024]{2,1,0:T(8,128)(2,1)}), bf16[4,64,1024]{2,1,0:T(8,128)(2,1)S(1)}, u32[]{:S(2)}, u32[]{:S(2)}) async-start(bf16[4,64,1024]{2,1,0:T(8,128)(2,1)} %bitcast.14), calls=%async_computation.3 | async-start | bytes 1048576 | tf_op jit(solution)/shard_map/all_to_all | solution.py:72
  78.1 26.7 %collective-permute-start.6 = (bf16[1024,512]{1,0:T(8,128)(2,1)}, bf16[1024,512]{1,0:T(8,128)(2,1)S(1)}, u32[]{:S(2)}, u32[]{:S(2)}) collective-permute-start(bf16[1024,512]{1,0:T(8,128)(2,1)} %bitcast.16), channel_id=1, source_target_pairs={{0,130},{2,128},{128,2},{130,0},{1,131},{3,129},{129,3},{131,1},{4... | collective-permute-start | bytes 3145736 | tf_op jit(solution)/shard_map/ppermute | solution.py:30
  78.6 22.9 %collective-permute-start.8 = (bf16[1024,512]{1,0:T(8,128)(2,1)}, bf16[1024,512]{1,0:T(8,128)(2,1)S(1)}, u32[]{:S(2)}, u32[]{:S(2)}) collective-permute-start(bf16[1024,512]{1,0:T(8,128)(2,1)} %bitcast.16), channel_id=1, source_target_pairs={{0,128},{128,0},{1,129},{129,1},{2,130},{130,2},{3,131},{131,3},{4... | collective-permute-start | bytes 3145736 | tf_op jit(solution)/shard_map/ppermute | solution.py:30
  87.5 20.1 %all-to-all-start.4 = ((bf16[4,64,2048]{2,1,0:T(8,128)(2,1)}), bf16[4,64,2048]{2,1,0:T(8,128)(2,1)S(1)}, u32[]{:S(2)}, u32[]{:S(2)}) async-start(bf16[4,64,2048]{2,1,0:T(8,128)(2,1)} %broadcast_in_dim.20), calls=%async_computation.4 | async-start | bytes 2097152 | tf_op jit(solution)/shard_map/all_to_all | solution.py:65
  91.2 111.8 %collective-permute-start.18 = (bf16[256,512]{1,0:T(8,128)(2,1)}, bf16[256,512]{1,0:T(8,128)(2,1)}, u32[]{:S(2)}, u32[]{:S(2)}) collective-permute-start(bf16[256,512]{1,0:T(8,128)(2,1)} %get-tuple-element.24), channel_id=1, source_target_pairs={{0,130},{2,128},{128,2},{130,0},{1,131},{3,129},{129,3},{131,1},{4... | collective-permute-start | bytes 786440 | tf_op jit(solution)/shard_map/ppermute | solution.py:30
  102.3 17.4 %collective-permute-start.9 = (bf16[512,512]{1,0:T(8,128)(2,1)}, bf16[512,512]{1,0:T(8,128)(2,1)}, u32[]{:S(2)}, u32[]{:S(2)}) collective-permute-start(bf16[512,512]{1,0:T(8,128)(2,1)} %slice.172), channel_id=1, source_target_pairs={{0,130},{2,128},{128,2},{130,0},{1,131},{3,129},{129,3},{131,1},{4... | collective-permute-start | bytes 1572872 | tf_op jit(solution)/shard_map/ppermute | solution.py:30
  105.6 15.4 %collective-permute-start.7 = (bf16[512,512]{1,0:T(8,128)(2,1)}, bf16[512,512]{1,0:T(8,128)(2,1)}, u32[]{:S(2)}, u32[]{:S(2)}) collective-permute-start(bf16[512,512]{1,0:T(8,128)(2,1)} %slice.170), channel_id=1, source_target_pairs={{0,128},{128,0},{1,129},{129,1},{2,130},{130,2},{3,131},{131,3},{4... | collective-permute-start | bytes 1572872 | tf_op jit(solution)/shard_map/ppermute | solution.py:30
  131.4 8.7 %all-to-all-start.6 = ((f32[4,1,2048]{2,1,0:T(1,128)}), f32[4,1,2048]{2,1,0:T(1,128)S(1)}, u32[]{:S(2)}, u32[]{:S(2)}) async-start(f32[4,1,2048]{2,1,0:T(1,128)} %broadcast_in_dim.23), calls=%async_computation.6 | async-start | bytes 65536 | tf_op jit(solution)/shard_map/all_to_all | solution.py:65
  140.7 12.7 %all-to-all-start.5 = ((f32[32,4,128]{2,1,0:T(4,128)}), f32[32,4,128]{2,1,0:T(4,128)S(1)}, u32[]{:S(2)}, u32[]{:S(2)}) async-start(f32[32,4,128]{2,1,0:T(4,128)} %broadcast_in_dim.22), calls=%async_computation.5 | async-start | bytes 131072 | tf_op jit(solution)/shard_map/all_to_all | solution.py:65
  145.7 57.8 %collective-permute-start.24 = (bf16[256,1024]{1,0:T(8,128)(2,1)}, bf16[256,1024]{1,0:T(8,128)(2,1)}, u32[]{:S(2)}, u32[]{:S(2)}) collective-permute-start(bf16[256,1024]{1,0:T(8,128)(2,1)} %get-tuple-element.19), channel_id=1, source_target_pairs={{0,130},{2,128},{128,2},{130,0},{1,131},{3,129},{129,3},{131,1},{4... | collective-permute-start | bytes 1572872 | tf_op jit(solution)/shard_map/ppermute | solution.py:30
  146.2 60.3 %collective-permute-start.23 = (bf16[256,1024]{1,0:T(8,128)(2,1)}, bf16[256,1024]{1,0:T(8,128)(2,1)}, u32[]{:S(2)}, u32[]{:S(2)}) collective-permute-start(bf16[256,1024]{1,0:T(8,128)(2,1)} %get-tuple-element.19), channel_id=1, source_target_pairs={{0,2},{2,0},{1,3},{3,1},{4,6},{6,4},{5,7},{7,5},{8,10},{10,8},{9,1... | collective-permute-start | bytes 1572872 | tf_op jit(solution)/shard_map/ppermute | solution.py:30
  146.2 60.9 %collective-permute-start.22 = (bf16[256,1024]{1,0:T(8,128)(2,1)}, bf16[256,1024]{1,0:T(8,128)(2,1)}, u32[]{:S(2)}, u32[]{:S(2)}) collective-permute-start(bf16[256,1024]{1,0:T(8,128)(2,1)} %get-tuple-element.18), channel_id=1, source_target_pairs={{0,128},{128,0},{1,129},{129,1},{2,130},{130,2},{3,131},{131,3},{4... | collective-permute-start | bytes 1572872 | tf_op jit(solution)/shard_map/ppermute | solution.py:30
  160.9 15.4 %all-to-all-start.7 = ((bf16[4,64,2048]{2,1,0:T(8,128)(2,1)}), bf16[4,64,2048]{2,1,0:T(8,128)(2,1)S(1)}, u32[]{:S(2)}, u32[]{:S(2)}) async-start(bf16[4,64,2048]{2,1,0:T(8,128)(2,1)} %pad_maximum_fusion), calls=%async_computation.7 | async-start | bytes 2097152 | tf_op jit(solution)/shard_map/all_to_all | solution.py:72
  177.8 14.1 %all-to-all-start.8 = ((bf16[4,64,2048]{2,1,0:T(8,128)(2,1)}), bf16[4,64,2048]{2,1,0:T(8,128)(2,1)S(1)}, u32[]{:S(2)}, u32[]{:S(2)}) async-start(bf16[4,64,2048]{2,1,0:T(8,128)(2,1)} %broadcast_in_dim.24), calls=%async_computation.8 | async-start | bytes 2097152 | tf_op jit(solution)/shard_map/all_to_all | solution.py:65
  202.3 8.7 %collective-permute-start.27 = (bf16[256,512]{1,0:T(8,128)(2,1)S(1)}, bf16[256,512]{1,0:T(8,128)(2,1)S(1)}, u32[]{:S(2)}, u32[]{:S(2)}) collective-permute-start(bf16[256,512]{1,0:T(8,128)(2,1)S(1)} %get-tuple-element.23), channel_id=1, source_target_pairs={{0,130},{2,128},{128,2},{130,0},{1,131},{3,129},{129,3},{131,1},{4... | collective-permute-start | bytes 786440 | tf_op jit(solution)/shard_map/ppermute | solution.py:30
  203.0 19.6 %collective-permute-start.25 = (bf16[256,512]{1,0:T(8,128)(2,1)S(1)}, bf16[256,512]{1,0:T(8,128)(2,1)}, u32[]{:S(2)}, u32[]{:S(2)}) collective-permute-start(bf16[256,512]{1,0:T(8,128)(2,1)S(1)} %get-tuple-element.23), channel_id=1, source_target_pairs={{0,128},{128,0},{1,129},{129,1},{2,130},{130,2},{3,131},{131,3},{4... | collective-permute-start | bytes 786440 | tf_op jit(solution)/shard_map/ppermute | solution.py:30
  203.5 17.4 %collective-permute-start.26 = (bf16[256,512]{1,0:T(8,128)(2,1)S(1)}, bf16[256,512]{1,0:T(8,128)(2,1)}, u32[]{:S(2)}, u32[]{:S(2)}) collective-permute-start(bf16[256,512]{1,0:T(8,128)(2,1)S(1)} %get-tuple-element.22), channel_id=1, source_target_pairs={{0,2},{2,0},{1,3},{3,1},{4,6},{6,4},{5,7},{7,5},{8,10},{10,8},{9,1... | collective-permute-start | bytes 786440 | tf_op jit(solution)/shard_map/ppermute | solution.py:30
  206.5 51.0 %collective-permute-start.21 = (bf16[256,1024]{1,0:T(8,128)(2,1)S(1)}, bf16[256,1024]{1,0:T(8,128)(2,1)S(1)}, u32[]{:S(2)}, u32[]{:S(2)}) collective-permute-start(bf16[256,1024]{1,0:T(8,128)(2,1)S(1)} %get-tuple-element.21), channel_id=1, source_target_pairs={{0,130},{2,128},{128,2},{130,0},{1,131},{3,129},{129,3},{131,1},{4... | collective-permute-start | bytes 1572872 | tf_op jit(solution)/shard_map/ppermute | solution.py:30
  207.1 50.4 %collective-permute-start.20 = (bf16[256,1024]{1,0:T(8,128)(2,1)S(1)}, bf16[256,1024]{1,0:T(8,128)(2,1)}, u32[]{:S(2)}, u32[]{:S(2)}) collective-permute-start(bf16[256,1024]{1,0:T(8,128)(2,1)S(1)} %get-tuple-element.21), channel_id=1, source_target_pairs={{0,2},{2,0},{1,3},{3,1},{4,6},{6,4},{5,7},{7,5},{8,10},{10,8},{9,1... | collective-permute-start | bytes 1572872 | tf_op jit(solution)/shard_map/ppermute | solution.py:30
  211.0 46.5 %collective-permute-start.19 = (bf16[256,1024]{1,0:T(8,128)(2,1)S(1)}, bf16[256,1024]{1,0:T(8,128)(2,1)}, u32[]{:S(2)}, u32[]{:S(2)}) collective-permute-start(bf16[256,1024]{1,0:T(8,128)(2,1)S(1)} %get-tuple-element.20), channel_id=1, source_target_pairs={{0,128},{128,0},{1,129},{129,1},{2,130},{130,2},{3,131},{131,3},{4... | collective-permute-start | bytes 1572872 | tf_op jit(solution)/shard_map/ppermute | solution.py:30
  211.7 18.0 %all-to-all-start.9 = ((bf16[8,128,128]{2,1,0:T(8,128)(2,1)}), bf16[8,128,128]{2,1,0:T(8,128)(2,1)S(1)}, u32[]{:S(2)}, u32[]{:S(2)}) async-start(bf16[8,128,128]{2,1,0:T(8,128)(2,1)} %bitcast.48), calls=%async_computation.9 | async-start | bytes 524288 | tf_op jit(solution)/shard_map/all_to_all | solution.py:219
  220.8 25.2 %collective-permute-start.17 = (bf16[256,512]{1,0:T(8,128)(2,1)S(1)}, bf16[256,512]{1,0:T(8,128)(2,1)}, u32[]{:S(2)}, u32[]{:S(2)}) collective-permute-start(bf16[256,512]{1,0:T(8,128)(2,1)S(1)} %copy-done.19), channel_id=1, source_target_pairs={{0,2},{2,0},{1,3},{3,1},{4,6},{6,4},{5,7},{7,5},{8,10},{10,8},{9,1... | collective-permute-start | bytes 786440 | tf_op jit(solution)/shard_map/ppermute | solution.py:30
  222.6 34.9 %collective-permute-start.16 = (bf16[256,512]{1,0:T(8,128)(2,1)S(1)}, bf16[256,512]{1,0:T(8,128)(2,1)S(1)}, u32[]{:S(2)}, u32[]{:S(2)}) collective-permute-start(bf16[256,512]{1,0:T(8,128)(2,1)S(1)} %copy-done.20), channel_id=1, source_target_pairs={{0,128},{128,0},{1,129},{129,1},{2,130},{130,2},{3,131},{131,3},{4... | collective-permute-start | bytes 786440 | tf_op jit(solution)/shard_map/ppermute | solution.py:30
  246.0 15.4 %collective-permute-start.15 = (bf16[128,128]{1,0:T(8,128)(2,1)S(1)}, bf16[128,128]{1,0:T(8,128)(2,1)S(1)}, u32[]{:S(2)}, u32[]{:S(2)}) collective-permute-start(bf16[128,128]{1,0:T(8,128)(2,1)S(1)} %reduce_sum.112), channel_id=1, source_target_pairs={{0,0},{1,32},{2,64},{3,96},{4,1},{5,33},{6,65},{7,97},{8,2},{9,34}... | collective-permute-start | bytes 98312 | tf_op jit(solution)/shard_map/ppermute | solution.py:30
  (27 other events, 223.8 us)

commit v2 on v1

v2 whole, which is shorter than its diff:
```python
import functools
import itertools

import jax
import jax.numpy as jnp
from jax import lax
from jax.experimental import pallas as pl
from jax.experimental.pallas import tpu as pltpu
from jax.sharding import Mesh, PartitionSpec as P


PENALTY = 0.5
SPREAD_FLOOR = 0.25
EPSILON = 1e-05
AXES = ("xl", "y", "z", "xh", "c")
SIZES = (2, 4, 8, 2, 2)
BF16 = jnp.bfloat16
F32 = jnp.float32


def permuted(array, axes, target):
    sizes = [SIZES[AXES.index(a)] for a in axes]

    def flat(place):
        index = 0
        for i, size in zip(place, sizes):
            index = index * size + i
        return index

    pairs = [
        (flat(place), flat(target(*place))) for place in itertools.product(*map(range, sizes))
    ]
    return lax.ppermute(array, axes, pairs)


def over_xl(array):
    return permuted(array, ("xl",), lambda xl: (1 - xl,))


def over_xh(array):
    return permuted(array, ("xh",), lambda xh: (1 - xh,))


def over_diagonal(array):
    return permuted(array, ("xl", "xh"), lambda xl, xh: (1 - xl, 1 - xh))


def over_cores(array):
    return permuted(array, ("c",), lambda c: (1 - c,))


def owner_of(xl, y, z, xh, c):
    return (xl, 2 * xh + c, ((z // 4) ^ xl) * 4 + y, (z % 4) // 2, z % 2)


def to_owner(array):
    return permuted(array, AXES, owner_of)


def from_owner(array):
    places = list(itertools.product(*map(range, SIZES)))
    back = {owner_of(*place): place for place in places}
    return permuted(array, AXES, lambda *place: back[place])


def exchanged(array, axes):
    return lax.all_to_all(array, axes, 0, 0, tiled=True)


def sent_to_all(array, axes):
    count = lax.axis_size(axes)
    return exchanged(jnp.broadcast_to(array[None], (count, *array.shape)), axes)


def to_reporter(array):
    return permuted(array, ("y", "xh", "c"), lambda y, xh, c: (2 * xh + c, y // 2, y % 2))


def pieces_over_y(partial):
    return exchanged(partial.reshape(SIZES[1], -1, partial.shape[1]), "y")


def gathered_over_y(copies):
    return exchanged(copies, "y").reshape(-1, copies.shape[-1])


def mul(left, right):
    return jnp.dot(left, right, preferred_element_type=F32)


def mul_t(left, right):
    return lax.dot_general(left, right, (((1,), (1,)), ((), ())), preferred_element_type=F32)


def t_mul(left, right):
    return lax.dot_general(left, right, (((0,), (0,)), ((), ())), preferred_element_type=F32)


def pooling(lengths, offsets, row_count):
    seq_ends = jnp.cumsum(lengths)
    seq_starts = seq_ends - lengths
    target = seq_starts + offsets % lengths
    places = jnp.arange(row_count, dtype=jnp.int32)[:, None]
    inside = jnp.logical_and(places >= seq_starts[None, :], places < seq_ends[None, :])
    marked = places == target[None, :]
    return inside.astype(F32) / lengths.astype(F32)[None, :] + marked.astype(F32)


def silu_slope(gate_in):
    sigmoided = jax.nn.sigmoid(gate_in)
    return sigmoided * (1.0 + gate_in * (1.0 - sigmoided))


VMEM = pl.BlockSpec(memory_space=pltpu.VMEM)
SMEM = pl.BlockSpec(memory_space=pltpu.SMEM)


def limit(mebibytes):
    return pltpu.CompilerParams(vmem_limit_bytes=mebibytes << 20)


def like(shape, dtype):
    return jax.ShapeDtypeStruct(shape, dtype)


def activate_kernel(parts_ref, gate_ref, copies_ref):
    step = 512
    for at in range(0, gate_ref.shape[1], step):
        cols = slice(at, at + step)
        gate = sum(parts_ref[k, :, cols].astype(F32) for k in range(parts_ref.shape[0]))
        gate_ref[:, cols] = gate
        activated = (gate * jax.nn.sigmoid(gate)).astype(BF16)
        for k in range(copies_ref.shape[0]):
            copies_ref[k, :, cols] = activated


def activate(parts):
    count, rows, width = parts.shape
    return pl.pallas_call(
        activate_kernel,
        out_shape=(like((rows, width), F32), like((count, rows, width), BF16)),
        in_specs=[VMEM],
        out_specs=(VMEM, VMEM),
        name="activate",
        compiler_params=limit(6),
    )(parts)


def gate_kernel(mine_ref, partner_ref, own, xl_a, xl_b, dg_a, dg_b, xh_a, xh_b, out_ref):
    half, units = xl_a.shape
    hid_o, hid_t = (jnp.concatenate([mine_ref[i], partner_ref[i]], axis=0) for i in range(2))
    out_ref[:, :units] = (
        mul(hid_o, own[...]) + mul(hid_t[:, :half], xl_a[...]) + mul(hid_t[:, half:], xl_b[...])
    ).astype(BF16)
    out_ref[:, units:] = (
        mul(hid_o[:, :half], xh_a[...])
        + mul(hid_o[:, half:], xh_b[...])
        + mul(hid_t[:, :half], dg_a[...])
        + mul(hid_t[:, half:], dg_b[...])
    ).astype(BF16)


def gate_parts(mine, partner, blocks):
    return pl.pallas_call(
        gate_kernel,
        out_shape=like((2 * mine.shape[1], 2 * blocks[0].shape[1]), BF16),
        in_specs=[VMEM] * 9,
        out_specs=VMEM,
        name="gate",
        compiler_params=limit(14),
    )(mine, partner, *blocks)


def branch_kernel(act_ref, own, xl_a, xl_b, dg_a, dg_b, xh_a, xh_b, away_ref, stay_ref):
    rows, half, units = stay_ref.shape[1], xl_a.shape[0], own.shape[0]
    first = (
        mul(act_ref[:, :units], own[...])
        + mul(act_ref[:, units : units + half], xh_a[...])
        + mul(act_ref[:, units + half :], xh_b[...])
    )
    away_ref[0] = first[rows:].astype(BF16)
    stay_ref[0] = first[:rows]
    second = (
        mul(act_ref[:, :half], xl_a[...])
        + mul(act_ref[:, half:units], xl_b[...])
        + mul(act_ref[:, units : units + half], dg_a[...])
        + mul(act_ref[:, units + half :], dg_b[...])
    )
    away_ref[1] = second[rows:].astype(BF16)
    stay_ref[1] = second[:rows]


def branch_of(act, blocks):
    half, width = act.shape[0] // 2, blocks[0].shape[1]
    return pl.pallas_call(
        branch_kernel,
        out_shape=(like((2, half, width), BF16), like((2, half, width), F32)),
        in_specs=[VMEM] * 8,
        out_specs=(VMEM, VMEM),
        name="branch",
        compiler_params=limit(14),
    )(act, *blocks)


def back_hidden_kernel(back_ref, own, xl_a, xl_b, dg_a, dg_b, xh_a, xh_b, away_ref, stay_ref):
    rows, half, units = stay_ref.shape[1], xl_a.shape[0], own.shape[1]
    back_o, back_t = back_ref[:, :units], back_ref[:, units:]

    def put(i, at, result):
        cols = slice(at, at + result.shape[1])
        away_ref[i, :, cols] = result[rows:].astype(BF16)
        stay_ref[i, :, cols] = result[:rows]

    put(0, 0, mul_t(back_o, own[:half]) + mul_t(back_t, xh_a[...]))
    put(0, half, mul_t(back_o, own[half:]) + mul_t(back_t, xh_b[...]))
    put(1, 0, mul_t(back_o, xl_a[...]) + mul_t(back_t, dg_a[...]))
    put(1, half, mul_t(back_o, xl_b[...]) + mul_t(back_t, dg_b[...]))


def back_hidden(back, blocks):
    half, width = back.shape[0] // 2, blocks[0].shape[0]
    return pl.pallas_call(
        back_hidden_kernel,
        out_shape=(like((2, half, width), BF16), like((2, half, width), F32)),
        in_specs=[VMEM] * 8,
        out_specs=(VMEM, VMEM),
        name="back_hidden",
        compiler_params=limit(14),
    )(back, *blocks)


def as_row(column):
    return jnp.transpose(jnp.broadcast_to(column, (column.shape[0], 128)))[0:1]


def as_columns(row):
    return jnp.transpose(jnp.broadcast_to(row, (128, row.shape[1])))


def combine_kernel(hidden_ref, stay_ref, got_ref, vec_ref, full_ref, half_ref, sums_ref):
    squares = products = 0.0
    for i in range(2):
        combined = hidden_ref[i].astype(F32) + stay_ref[i] + got_ref[i].astype(F32)
        full_ref[i] = combined
        half_ref[i] = combined.astype(BF16)
        squares += jnp.sum(combined * combined, axis=1, keepdims=True)
        products += jnp.sum(combined * vec_ref[i : i + 1], axis=1, keepdims=True)
    sums_ref[0:1] = as_row(squares)
    sums_ref[1:2] = as_row(products)


def combine(hidden, stay, got, vec):
    return pl.pallas_call(
        combine_kernel,
        out_shape=(like(stay.shape, F32), like(stay.shape, BF16), like((2, stay.shape[1]), F32)),
        in_specs=[VMEM] * 4,
        out_specs=(VMEM,) * 3,
        name="combine",
        compiler_params=limit(6),
    )(hidden, stay, got, vec)


def rows_of(values, count):
    width = values[0].shape[1]
    index = lax.broadcasted_iota(jnp.int32, (count, width), 0)
    stacked = jnp.zeros((count, width), F32)
    for i, value in enumerate(values):
        stacked = jnp.where(index == i, jnp.broadcast_to(value, (count, width)), stacked)
    return stacked


def against_kernel(
    place_ref, own_ref, partner_ref, vec_ref, own, xl_a, xl_b, dg_a, dg_b, xh_a, xh_b,
    out_0, out_1, out_2, out_3, both, left,
):
    outs = (out_0, out_1, out_2, out_3)
    rows, half, units = own_ref.shape[1], xl_a.shape[0], own.shape[0]
    piece = 2 * rows // len(outs)
    for i in range(2):
        both[i, :rows] = own_ref[i]
        both[i, rows:] = partner_ref[i]
        for k in range(len(outs)):
            start = pl.multiple_of(((place_ref[0] + k) % len(outs)) * piece, piece)
            left[i, k * piece : (k + 1) * piece] = both[i, pl.ds(start, piece), :]
        vec = vec_ref[i : i + 1]
        high = vec.astype(BF16).astype(F32)
        middle = (vec - high).astype(BF16).astype(F32)
        left[i, 2 * rows :] = rows_of((high, middle, vec - high - middle), 16).astype(BF16)

    def put(result, at):
        vec = jnp.sum(result[2 * rows :], axis=0, keepdims=True)
        high = vec.astype(BF16).astype(F32)
        extra = rows_of((high, vec - high), 8).astype(BF16)
        for k, out in enumerate(outs):
            cols = slice(at, at + result.shape[1])
            out[:piece, cols] = result[k * piece : (k + 1) * piece].astype(BF16)
            out[piece:, cols] = extra

    put(mul_t(left[0], own[:half]) + mul_t(left[1], xl_a[...]), 0)
    put(mul_t(left[0], own[half:]) + mul_t(left[1], xl_b[...]), half)
    put(mul_t(left[0], xh_a[...]) + mul_t(left[1], dg_a[...]), units)
    put(mul_t(left[0], xh_b[...]) + mul_t(left[1], dg_b[...]), units + half)


def against_out(place, own, partner, vec, blocks):
    units, width = blocks[0].shape
    rows = own.shape[1]
    return pl.pallas_call(
        against_kernel,
        out_shape=(like((2 * rows // 4 + 8, 2 * units), BF16),) * 4,
        in_specs=[SMEM] + [VMEM] * 10,
        out_specs=(VMEM,) * 4,
        scratch_shapes=[
            pltpu.VMEM((2, 2 * rows, width), BF16),
            pltpu.VMEM((2, 2 * rows + 16, width), BF16),
        ],
        name="against_out",
        compiler_params=limit(14),
    )(place, own, partner, vec, *blocks)


def back_kernel(
    place_ref, weight_ref, every_ref, pooler_ref, gate_ref, part_0, part_1, part_2, part_3,
    copies_ref, by_vec_ref, by_combined_ref, penalized_ref, *, features,
):
    members, rows = every_ref.shape[1], every_ref.shape[3]
    heads = lax.broadcasted_iota(jnp.int32, (members, 1), 0)
    lanes = lax.broadcasted_iota(jnp.int32, (1, 128), 1)
    mine = heads == place_ref[1]

    def of_mine(values):
        return jnp.sum(jnp.where(mine, values, 0.0), axis=0, keepdims=True)

    penalized = jnp.zeros((1, 128), F32)
    for slab in range(2):
        squares, products = (
            sum(every_ref[k, :, 2 * slab + i, :] for k in range(every_ref.shape[0]))
            for i in range(2)
        )
        inverse = lax.rsqrt(squares / features + EPSILON)
        scores = products * inverse
        tok_weight = jnp.zeros((1, rows), F32)
        for s in range(pooler_ref.shape[1]):
            pool = pooler_ref[slab, s : s + 1, :]
            rewards = jnp.sum(scores * pool, axis=1, keepdims=True)
            center = jnp.sum(rewards, axis=0, keepdims=True) / members
            spread = jnp.sum((rewards - center) ** 2, axis=0, keepdims=True) / members
            deviation = jnp.sqrt(spread + SPREAD_FLOOR)
            if slab == 0:
                penalized = jnp.where(lanes == s, center - PENALTY * deviation, penalized)
            pull = 1.0 - PENALTY * (of_mine(rewards) - center) / deviation
            weight = weight_ref[slab * pooler_ref.shape[1] + s] / members
            tok_weight += weight * pull * pool
        inverse, scores = of_mine(inverse), of_mine(scores)
        at = slice(slab * rows, (slab + 1) * rows)
        by_vec_ref[at] = as_columns(tok_weight * inverse)
        by_combined_ref[at] = as_columns(tok_weight * scores * inverse * inverse / features)
    penalized_ref[...] = penalized
    piece = gate_ref.shape[0]
    start = pl.multiple_of(place_ref[0] * piece, piece)
    by_vec = by_vec_ref[pl.ds(start, piece), 0:1]
    by_combined = by_combined_ref[pl.ds(start, piece), 0:1]
    parts = (part_0, part_1, part_2, part_3)
    step = 512
    for at in range(0, gate_ref.shape[1], step):
        cols = slice(at, at + step)
        combined_out = sum(part[:piece, cols].astype(F32) for part in parts)
        vec_out = jnp.sum(
            sum(part[piece:, cols].astype(F32) for part in parts), axis=0, keepdims=True
        )
        raw = by_vec * vec_out - by_combined * combined_out
        back = (raw * silu_slope(gate_ref[:, cols])).astype(BF16)
        for k in range(copies_ref.shape[0]):
            copies_ref[k, :, cols] = back


def back_of(place, weight, every, pooler, gate, parts, features):
    piece, width = gate.shape
    rows = every.shape[3]
    return pl.pallas_call(
        functools.partial(back_kernel, features=features),
        out_shape=(
            like((4, piece, width), BF16),
            like((2 * rows, 128), F32),
            like((2 * rows, 128), F32),
            like((1, 128), F32),
        ),
        in_specs=[SMEM, SMEM] + [VMEM] * 7,
        out_specs=(VMEM,) * 4,
        name="back",
        compiler_params=limit(8),
    )(place, weight, every, pooler, gate, *parts)


def local(hidden, w_in, w_out, score_vec, lengths, reward_offset, seq_weight):
    xl, y, z, xh, c = (lax.axis_index(a) for a in AXES)
    rows, members, features = 128, SIZES[2], 4096
    mine = from_owner(hidden)

    def ring_blocks(block):
        top, bottom = jnp.split(block, 2)
        dg_a, xl_b = over_diagonal(top), over_xl(bottom)
        xl_a, dg_b = over_xl(top), over_diagonal(bottom)
        xh_a, xh_b = over_xl(dg_a), over_diagonal(xl_b)
        return block, xl_a, xl_b, dg_a, dg_b, xh_a, xh_b

    w_blocks, v_blocks = ring_blocks(w_in[0]), ring_blocks(w_out[0])
    blocks = sent_to_all(mine, "z").reshape(2, 4, rows, -1)
    slab_mine = jnp.moveaxis(blocks, 1, 2).reshape(2, rows, -1)
    slab_partner = over_cores(slab_mine)
    gate, copies = activate(pieces_over_y(gate_parts(slab_mine, slab_partner, w_blocks)))
    units = gate.shape[1] // 2
    activated = gathered_over_y(copies)
    act_o, act_t = activated[:, :units], activated[:, units:]
    facts = jnp.concatenate([lengths.astype(F32), reward_offset.astype(F32), seq_weight])
    turns = [facts] + [
        permuted(facts, ("y",), lambda i, k=k: ((i + k) % SIZES[1],))
        for k in range(1, SIZES[1])
    ]
    turns = jnp.stack(turns)
    poolers, pulls = [], []
    for slab in (2 * xh + c, 2 * xh + 1 - c):
        of_slab = lax.dynamic_index_in_dim(turns, (y - slab) % SIZES[1], 0, keepdims=False)
        poolers.append(pooling(of_slab[0].astype(jnp.int32), of_slab[1].astype(jnp.int32), rows).T)
        pulls.append(of_slab[2])
    pooler, weight = jnp.stack(poolers), jnp.concatenate(pulls)
    width = slab_mine.shape[2]
    vec = jnp.stack(
        [
            lax.dynamic_slice_in_dim(score_vec[0], (4 * xl + y) * width, width),
            lax.dynamic_slice_in_dim(score_vec[0], (4 * (1 - xl) + y) * width, width),
        ]
    )
    away, stay = branch_of(activated, v_blocks)
    combined, combined_half, sums = combine(slab_mine, stay, over_cores(away), vec)
    combined_partner = over_cores(combined_half)
    place = jnp.stack([y, z]).astype(jnp.int32)
    parts = against_out(place, combined_half, combined_partner, vec, v_blocks)
    parts = [parts[0]] + [
        permuted(parts[k], ("y",), lambda i, k=k: ((i + k) % SIZES[1],))
        for k in range(1, SIZES[1])
    ]
    sums = jnp.concatenate([sums, over_cores(sums)])
    every = sent_to_all(sums, ("y", "z")).reshape(SIZES[1], members, 4, rows)
    copies, by_vec, by_combined, penalized = back_of(
        place, weight, every, pooler, gate, parts, features
    )
    by_vec, by_combined = by_vec[:, :1], by_combined[:, :1]
    combined_both = jnp.concatenate([combined_half, combined_partner], axis=1)
    slopes = (by_vec * vec[:, None] - by_combined * combined_both.astype(F32)).astype(BF16)

    def quarters(own, by_xl, by_xh, by_diagonal):
        return (own, over_xl(by_xl), over_xh(by_xh), over_diagonal(by_diagonal))

    act_all = quarters(act_o, act_o, act_t, act_t)
    back_gate = gathered_over_y(copies)
    slope_all = quarters(slopes[0], slopes[1], slopes[0], slopes[1])
    hid_o, hid_t = jnp.concatenate([slab_mine, slab_partner], axis=1)
    hid_all = quarters(hid_o, hid_t, hid_o, hid_t)
    back_o, back_t = back_gate[:, :units], back_gate[:, units:]
    back_all = quarters(back_o, back_o, back_t, back_t)
    away, stay = back_hidden(back_gate, w_blocks)
    direct = by_vec[:rows] * vec[:, None] - by_combined[:rows] * combined
    term = direct + stay + over_cores(away).astype(F32)
    parts = jnp.moveaxis(term.astype(BF16).reshape(2, rows, 4, -1), 2, 1).reshape(8, rows, -1)
    from_heads = exchanged(parts, "z")
    block = jnp.sum(from_heads.astype(F32), axis=0)
    grad_hidden = to_owner(block.astype(BF16)).astype(F32)
    reported = to_reporter(penalized[:, : lengths.shape[1]])
    grad_out = t_mul(jnp.concatenate(act_all), jnp.concatenate(slope_all))
    grad_in = t_mul(jnp.concatenate(hid_all), jnp.concatenate(back_all))
    return (reported, grad_hidden, grad_in[None], grad_out[None])


def solution(mesh):
    fine = Mesh(mesh.devices.reshape(SIZES), AXES)
    dp, member, mp = ("xl", "y"), "z", ("xh", "c")
    in_specs = (
        P(dp, (member, *mp)),
        P(member, dp, mp),
        P(member, mp, dp),
        P(member, None),
        P(dp, None),
        P(dp, None),
        P(dp, None),
    )
    out_specs = (
        P(dp, None),
        P(dp, (member, *mp)),
        P(member, dp, mp),
        P(member, mp, dp),
    )
    return jax.shard_map(local, mesh=fine, in_specs=in_specs, out_specs=out_specs, check_vma=False)
```

time: 264 us -> 240 us (0.909)
  the two profiles are of different devices: /device:TPU:7 before, /device:TPU:70 now
where the time goes in v2:
time: 240 us; the launch traced here: 239 us
  waiting for transfers between devices  91 us (38%)
  starting transfers between devices  89.4 us (37%)
  local copies, waits for them, and re-layouts  31.4 us (13%)
  Pallas kernels  13.8 us (6%)
  matrix products  8.05 us (3%)
  other arithmetic  3.59 us (1%)
    ppermute x38, waiting for transfers between devices, permuted(): return lax.ppermute(array, axes, pairs)  70.9 us
    ppermute x38, starting transfers between devices, permuted(): return lax.ppermute(array, axes, pairs)  56.9 us
    all_to_all x6, starting transfers between devices, exchanged(): return lax.all_to_all(array, axes, 0, 0, tiled=True)  32.4 us
    all_to_all x6, waiting for transfers between devices, exchanged(): return lax.all_to_all(array, axes, 0, 0, tiled=True)  20.2 us
    unnamed x92, local copies, waits for them, and re-layouts  19.9 us
    dot_general x2, matrix products, t_mul(): lax.dot_general(left, right, (((0,), (0,)), ((), ())), preferred_element_...  8.05 us
  transfers between devices with their start and end apart: 44, of which 16 were waited for; matrix products, arithmetic and copies ran while one was open for 8% of the time, Pallas kernels for 5%

profile of v2, /device:TPU:70, one launch (start us, length us, event | category | flops | bytes accessed | tf_op | source)
XLA Modules:
  0.0 238.6 jit_solution(10550118168060924857)
XLA Ops:
  0.7 2.3 slice_bitcast_fusion.2
  4.4 12.7 %collective-permute-start.3 = (bf16[128,128]{1,0:T(8,128)(2,1)S(1)}, bf16[128,128]{1,0:T(8,128)(2,1)S(1)}, u32[]{:S(2)}, u32[]{:S(2)}) collective-permute-start(bf16[128,128]{1,0:T(8,128)(2,1)S(1)} %copy-done.42), channel_id=1, source_target_pairs={{0,0},{1,4},{2,8},{3,12},{4,32},{5,36},{6,40},{7,44},{8,64},{9,68}... | collective-permute-start | bytes 98312 | tf_op jit(solution)/shard_map/ppermute | solution.py:33
  19.4 8.4 %all-to-all-start = ((bf16[8,128,128]{2,1,0:T(8,128)(2,1)}), bf16[8,128,128]{2,1,0:T(8,128)(2,1)S(1)}, u32[]{:S(2)}, u32[]{:S(2)}) async-start(bf16[8,128,128]{2,1,0:T(8,128)(2,1)} %broadcast_in_dim.8), calls=%async_computation | async-start | bytes 524288 | tf_op jit(solution)/shard_map/all_to_all | solution.py:67
  27.7 4.3 %collective-permute-start.5 = (bf16[256,1024]{1,0:T(8,128)(2,1)}, bf16[256,1024]{1,0:T(8,128)(2,1)}, u32[]{:S(2)}, u32[]{:S(2)}) collective-permute-start(bf16[256,1024]{1,0:T(8,128)(2,1)} %get-tuple-element.49), channel_id=1, source_target_pairs={{0,128},{128,0},{1,129},{129,1},{2,130},{130,2},{3,131},{131,3},{4... | collective-permute-start | bytes 1572872 | tf_op jit(solution)/shard_map/ppermute | solution.py:33
  32.1 3.2 %collective-permute-start.10 = (bf16[256,1024]{1,0:T(8,128)(2,1)S(1)}, bf16[256,1024]{1,0:T(8,128)(2,1)}, u32[]{:S(2)}, u32[]{:S(2)}) collective-permute-start(bf16[256,1024]{1,0:T(8,128)(2,1)S(1)} %collective-permute-done.6.xl_b), channel_id=1, source_target_pairs={{0,130},{2,128},{128,2},{130,0},{1,131},{3,129},{129,3},{131,1},{4... | collective-permute-start | bytes 1572872 | tf_op jit(solution)/shard_map/ppermute | solution.py:33
  38.3 6.8 %collective-permute-done.5.xl_a = bf16[256,1024]{1,0:T(8,128)(2,1)} collective-permute-done((bf16[256,1024]{1,0:T(8,128)(2,1)}, bf16[256,1024]{1,0:T(8,128)(2,1)}, u32[]{:S(2)}, u32[]{:S(2)}) %collective-permute-start.5) | collective-permute-done | bytes 524320 | tf_op jit(solution)/shard_map/ppermute | solution.py:33
  45.1 3.2 %collective-permute-done.8.dg_b = bf16[256,1024]{1,0:T(8,128)(2,1)} collective-permute-done((bf16[256,1024]{1,0:T(8,128)(2,1)}, bf16[256,1024]{1,0:T(8,128)(2,1)}, u32[]{:S(2)}, u32[]{:S(2)}) %collective-permute-start.8) | collective-permute-done | bytes 524320 | tf_op jit(solution)/shard_map/ppermute | solution.py:33
  48.4 6.4 %collective-permute-done.9.xh_a = bf16[256,1024]{1,0:T(8,128)(2,1)} collective-permute-done((bf16[256,1024]{1,0:T(8,128)(2,1)S(1)}, bf16[256,1024]{1,0:T(8,128)(2,1)}, u32[]{:S(2)}, u32[]{:S(2)}) %collective-permute-start.9) | collective-permute-done | bytes 524320 | tf_op jit(solution)/shard_map/ppermute | solution.py:33
  57.8 2.8 %gate.1 = bf16[256,2048]{1,0:T(8,128)(2,1)S(1)} custom-call(bf16[2,128,512]{2,1,0:T(8,128)(2,1)S(1)} %bitcast.82, bf16[2,128,512]{2,1,0:T(8,128)(2,1)S(1)} %collective-permute-done.4.partner_ref, bf16[512,1024]{1,0:T(8,128)(2,1)S(1)} %bitcast.78, bf16[256,1024]{1,0:T(8,128)(2,1)} %collective-permute-done.5.xl_a, ...), custom_call_target="tpu_custom_call" | custom-call | tf_op jit(solution)/shard_map/gate/pallas_call | solution.py:164
  61.6 3.5 %all-to-all-start.1 = ((bf16[4,64,2048]{2,1,0:T(8,128)(2,1)}), bf16[4,64,2048]{2,1,0:T(8,128)(2,1)S(1)}, u32[]{:S(2)}, u32[]{:S(2)}) async-start(bf16[4,64,2048]{2,1,0:T(8,128)(2,1)} %bitcast.80), calls=%async_computation.1 | async-start | bytes 2097152 | tf_op jit(solution)/shard_map/all_to_all | solution.py:67
  66.0 3.0 %collective-permute-start.14 = (bf16[512,512]{1,0:T(8,128)(2,1)}, bf16[512,512]{1,0:T(8,128)(2,1)}, u32[]{:S(2)}, u32[]{:S(2)}) collective-permute-start(bf16[512,512]{1,0:T(8,128)(2,1)} %get-tuple-element.46), channel_id=1, source_target_pairs={{0,130},{2,128},{128,2},{130,0},{1,131},{3,129},{129,3},{131,1},{4... | collective-permute-start | bytes 1572872 | tf_op jit(solution)/shard_map/ppermute | solution.py:33
  69.1 9.6 %all-to-all-done.1.parts_ref = bf16[4,64,2048]{2,1,0:T(8,128)(2,1)S(1)} async-done(((bf16[4,64,2048]{2,1,0:T(8,128)(2,1)}), bf16[4,64,2048]{2,1,0:T(8,128)(2,1)S(1)}, u32[]{:S(2)}, u32[]{:S(2)}) %all-to-all-start.1) | async-done | bytes 1048608 | tf_op jit(solution)/shard_map/all_to_all | solution.py:67
  80.7 3.5 %all-to-all-start.2 = ((bf16[4,64,2048]{2,1,0:T(8,128)(2,1)}), bf16[4,64,2048]{2,1,0:T(8,128)(2,1)S(1)}, u32[]{:S(2)}, u32[]{:S(2)}) async-start(bf16[4,64,2048]{2,1,0:T(8,128)(2,1)} %copy-done.13), calls=%async_computation.2 | async-start | bytes 2097152 | tf_op jit(solution)/shard_map/all_to_all | solution.py:67
  84.8 2.9 %collective-permute-start.16 = (bf16[512,512]{1,0:T(8,128)(2,1)}, bf16[512,512]{1,0:T(8,128)(2,1)S(1)}, u32[]{:S(2)}, u32[]{:S(2)}) collective-permute-start(bf16[512,512]{1,0:T(8,128)(2,1)} %collective-permute-done.12.xl_b), channel_id=1, source_target_pairs={{0,130},{2,128},{128,2},{130,0},{1,131},{3,129},{129,3},{131,1},{4... | collective-permute-start | bytes 1572872 | tf_op jit(solution)/shard_map/ppermute | solution.py:33
  87.9 7.8 %collective-permute-done.15.xh_a = bf16[512,512]{1,0:T(8,128)(2,1)S(1)} collective-permute-done((bf16[512,512]{1,0:T(8,128)(2,1)}, bf16[512,512]{1,0:T(8,128)(2,1)S(1)}, u32[]{:S(2)}, u32[]{:S(2)}) %collective-permute-start.15) | collective-permute-done | bytes 524320 | tf_op jit(solution)/shard_map/ppermute | solution.py:33
  100.2 2.8 %branch.1 = (bf16[2,128,512]{2,1,0:T(8,128)(2,1)S(1)}, f32[2,128,512]{2,1,0:T(8,128)S(1)}) custom-call(bf16[256,2048]{1,0:T(8,128)(2,1)S(1)} %bitcast.72, bf16[1024,512]{1,0:T(8,128)(2,1)S(1)} %bitcast.76, bf16[512,512]{1,0:T(8,128)(2,1)} %collective-permute-done.11.xl_a, bf16[512,512]{1,0:T(8,128)(2,1)} %collective-permute-done.12.xl_b, ...), custom_call_target="tpu_custom_call" | custom-call | tf_op jit(solution)/shard_map/branch/pallas_call | solution.py:195
  107.1 2.4 %collective-permute-start.28 = (bf16[256,512]{1,0:T(8,128)(2,1)}, bf16[256,512]{1,0:T(8,128)(2,1)}, u32[]{:S(2)}, u32[]{:S(2)}) collective-permute-start(bf16[256,512]{1,0:T(8,128)(2,1)} %get-tuple-element.53), channel_id=1, source_target_pairs={{0,130},{2,128},{128,2},{130,0},{1,131},{3,129},{129,3},{131,1},{4... | collective-permute-start | bytes 786440 | tf_op jit(solution)/shard_map/ppermute | solution.py:33
  109.5 3.9 %against_out.1 = (bf16[72,2048]{1,0:T(8,128)(2,1)S(1)}, bf16[72,2048]{1,0:T(8,128)(2,1)}, bf16[72,2048]{1,0:T(8,128)(2,1)}, bf16[72,2048]{1,0:T(8,128)(2,1)}) custom-call(s32[2]{0:T(128)S(1)} %pad_add_fusion.place_ref, bf16[2,128,512]{2,1,0:T(8,128)(2,1)S(1)} %get-tuple-element.26.own_ref, bf16[2,128,512]{2,1,0:T(8,128)(2,1)S(1)} %collective-permute-done.19.partner_ref, ...), custom_call_target="tpu_custom_call" | custom-call | tf_op jit(solution)/shard_map/against_out/pallas_call | solution.py:308
  115.9 2.7 %collective-permute-start.21 = (bf16[72,2048]{1,0:T(8,128)(2,1)}, bf16[72,2048]{1,0:T(8,128)(2,1)S(1)}, u32[]{:S(2)}, u32[]{:S(2)}) collective-permute-start(bf16[72,2048]{1,0:T(8,128)(2,1)} %get-tuple-element.29), channel_id=1, source_target_pairs={{0,64},{32,96},{64,0},{96,32},{1,65},{33,97},{65,1},{97,33},{2,66}... | collective-permute-start | bytes 884744 | tf_op jit(solution)/shard_map/ppermute | solution.py:33
  120.6 7.4 %all-to-all-start.3 = ((f32[32,4,128]{2,1,0:T(4,128)}), f32[32,4,128]{2,1,0:T(4,128)S(1)}, u32[]{:S(2)}, u32[]{:S(2)}) async-start(f32[32,4,128]{2,1,0:T(4,128)} %broadcast_in_dim.9), calls=%async_computation.3 | async-start | bytes 131072 | tf_op jit(solution)/shard_map/all_to_all | solution.py:67
  146.7 3.6 %all-to-all-start.4 = ((bf16[4,64,2048]{2,1,0:T(8,128)(2,1)}), bf16[4,64,2048]{2,1,0:T(8,128)(2,1)S(1)}, u32[]{:S(2)}, u32[]{:S(2)}) async-start(bf16[4,64,2048]{2,1,0:T(8,128)(2,1)} %copy-done.14), calls=%async_computation.4 | async-start | bytes 2097152 | tf_op jit(solution)/shard_map/all_to_all | solution.py:67
  154.6 8.9 %all-to-all-done.4 = bf16[4,64,2048]{2,1,0:T(8,128)(2,1)S(1)} async-done(((bf16[4,64,2048]{2,1,0:T(8,128)(2,1)}), bf16[4,64,2048]{2,1,0:T(8,128)(2,1)S(1)}, u32[]{:S(2)}, u32[]{:S(2)}) %all-to-all-start.4) | async-done | bytes 1048608 | tf_op jit(solution)/shard_map/all_to_all | solution.py:67
  163.4 2.8 %back_hidden.1 = (bf16[2,128,512]{2,1,0:T(8,128)(2,1)S(1)}, f32[2,128,512]{2,1,0:T(8,128)S(1)}) custom-call(bf16[256,2048]{1,0:T(8,128)(2,1)S(1)} %bitcast.74, bf16[512,1024]{1,0:T(8,128)(2,1)S(1)} %bitcast.79, bf16[256,1024]{1,0:T(8,128)(2,1)} %collective-permute-done.5.xl_a, bf16[256,1024]{1,0:T(8,128)(2,1)S(1)} %copy-done.6, ...), custom_call_target="tpu_custom_call" | custom-call | tf_op jit(solution)/shard_map/back_hidden/pallas_call | solution.py:222
  169.1 3.8 %collective-permute-start.36 = (bf16[256,512]{1,0:T(8,128)(2,1)S(1)}, bf16[256,512]{1,0:T(8,128)(2,1)}, u32[]{:S(2)}, u32[]{:S(2)}) collective-permute-start(bf16[256,512]{1,0:T(8,128)(2,1)S(1)} %copy-done.38), channel_id=1, source_target_pairs={{0,2},{2,0},{1,3},{3,1},{4,6},{6,4},{5,7},{7,5},{8,10},{10,8},{9,1... | collective-permute-start | bytes 786440 | tf_op jit(solution)/shard_map/ppermute | solution.py:33
  175.0 9.7 %collective-permute-done.23 = f32[1,4]{1,0:T(1,128)S(1)} collective-permute-done((f32[1,4]{1,0:T(1,128)S(1)}, f32[1,4]{1,0:T(1,128)S(1)}, u32[]{:S(2)}, u32[]{:S(2)}) %collective-permute-start.23) | collective-permute-done | bytes 48 | tf_op jit(solution)/shard_map/ppermute | solution.py:33
  185.5 6.0 %all-to-all-start.5 = ((bf16[8,128,128]{2,1,0:T(8,128)(2,1)}), bf16[8,128,128]{2,1,0:T(8,128)(2,1)S(1)}, u32[]{:S(2)}, u32[]{:S(2)}) async-start(bf16[8,128,128]{2,1,0:T(8,128)(2,1)} %bitcast.28), calls=%async_computation.5 | async-start | bytes 524288 | tf_op jit(solution)/shard_map/all_to_all | solution.py:67
  191.5 2.0 collective-permute-start.26
  193.6 3.4 %collective-permute-start.27 = (bf16[256,512]{1,0:T(8,128)(2,1)S(1)}, bf16[256,512]{1,0:T(8,128)(2,1)S(1)}, u32[]{:S(2)}, u32[]{:S(2)}) collective-permute-start(bf16[256,512]{1,0:T(8,128)(2,1)S(1)} %copy-done.37), channel_id=1, source_target_pairs={{0,2},{2,0},{1,3},{3,1},{4,6},{6,4},{5,7},{7,5},{8,10},{10,8},{9,1... | collective-permute-start | bytes 786440 | tf_op jit(solution)/shard_map/ppermute | solution.py:33
  197.0 4.3 %fusion.16 = f32[1,1024,512]{2,1,0:T(8,128)} fusion(bf16[256,1024]{1,0:T(8,128)(2,1)} %collective-permute-done.34, bf16[256,1024]{1,0:T(8,128)(2,1)} %collective-permute-done.33, bf16[256,1024]{1,0:T(8,128)(2,1)} %collective-permute-done.32, bf16[256,1024]{1,0:T(8,128)(2,1)} %get-tuple-element.42, bf16[256,512]{1,0:T(8,128)(2,1)} %copy-done.41, ...), kind=kOutput, calls=%fused_computation.16 | convolution fusion | flops 1086324736 | bytes 5242880 | tf_op jit(solution)/shard_map/dot_general | solution.py:96
  201.4 21.6 %collective-permute-done.27 = bf16[256,512]{1,0:T(8,128)(2,1)S(1)} collective-permute-done((bf16[256,512]{1,0:T(8,128)(2,1)S(1)}, bf16[256,512]{1,0:T(8,128)(2,1)S(1)}, u32[]{:S(2)}, u32[]{:S(2)}) %collective-permute-start.27) | collective-permute-done | bytes 262176 | tf_op jit(solution)/shard_map/ppermute | solution.py:33
  224.9 3.7 %fusion.19 = f32[1,512,1024]{2,1,0:T(8,128)} fusion(bf16[256,1024]{1,0:T(8,128)(2,1)S(1)} %collective-permute-done.31, bf16[256,1024]{1,0:T(8,128)(2,1)S(1)} %collective-permute-done.30, bf16[256,1024]{1,0:T(8,128)(2,1)} %collective-permute-done.29, bf16[256,1024]{1,0:T(8,128)(2,1)S(1)} %get-tuple-element.44, bf16[256,512]{1,0:T(8,128)(2,1)} %collective-permute-done.28, ...), kind=kOutput, calls=%fused_computation.17 | convolution fusion | flops 1086324736 | bytes 5242880 | tf_op jit(solution)/shard_map/dot_general | solution.py:96
  228.6 8.8 %collective-permute-done.25 = bf16[128,128]{1,0:T(8,128)(2,1)S(1)} collective-permute-done((bf16[128,128]{1,0:T(8,128)(2,1)S(1)}, bf16[128,128]{1,0:T(8,128)(2,1)S(1)}, u32[]{:S(2)}, u32[]{:S(2)}) %collective-permute-start.25) | collective-permute-done | bytes 32800 | tf_op jit(solution)/shard_map/ppermute | solution.py:33
  (195 shorter events, 59.0 us)
Async XLA Ops:
  3.0 29.0 %collective-permute-start.7 = (bf16[256,1024]{1,0:T(8,128)(2,1)}, bf16[256,1024]{1,0:T(8,128)(2,1)S(1)}, u32[]{:S(2)}, u32[]{:S(2)}) collective-permute-start(bf16[256,1024]{1,0:T(8,128)(2,1)} %get-tuple-element.49), channel_id=1, source_target_pairs={{0,130},{2,128},{128,2},{130,0},{1,131},{3,129},{129,3},{131,1},{4... | collective-permute-start | bytes 1572872 | tf_op jit(solution)/shard_map/ppermute | solution.py:33
  3.5 28.6 %collective-permute-start.6 = (bf16[256,1024]{1,0:T(8,128)(2,1)}, bf16[256,1024]{1,0:T(8,128)(2,1)S(1)}, u32[]{:S(2)}, u32[]{:S(2)}) collective-permute-start(bf16[256,1024]{1,0:T(8,128)(2,1)} %get-tuple-element.48), channel_id=1, source_target_pairs={{0,128},{128,0},{1,129},{129,1},{2,130},{130,2},{3,131},{131,3},{4... | collective-permute-start | bytes 1572872 | tf_op jit(solution)/shard_map/ppermute | solution.py:33
  19.4 16.1 %all-to-all-start = ((bf16[8,128,128]{2,1,0:T(8,128)(2,1)}), bf16[8,128,128]{2,1,0:T(8,128)(2,1)S(1)}, u32[]{:S(2)}, u32[]{:S(2)}) async-start(bf16[8,128,128]{2,1,0:T(8,128)(2,1)} %broadcast_in_dim.8), calls=%async_computation | async-start | bytes 524288 | tf_op jit(solution)/shard_map/all_to_all | solution.py:67
  27.7 17.4 %collective-permute-start.5 = (bf16[256,1024]{1,0:T(8,128)(2,1)}, bf16[256,1024]{1,0:T(8,128)(2,1)}, u32[]{:S(2)}, u32[]{:S(2)}) collective-permute-start(bf16[256,1024]{1,0:T(8,128)(2,1)} %get-tuple-element.49), channel_id=1, source_target_pairs={{0,128},{128,0},{1,129},{129,1},{2,130},{130,2},{3,131},{131,3},{4... | collective-permute-start | bytes 1572872 | tf_op jit(solution)/shard_map/ppermute | solution.py:33
  32.0 16.3 %collective-permute-start.8 = (bf16[256,1024]{1,0:T(8,128)(2,1)}, bf16[256,1024]{1,0:T(8,128)(2,1)}, u32[]{:S(2)}, u32[]{:S(2)}) collective-permute-start(bf16[256,1024]{1,0:T(8,128)(2,1)} %get-tuple-element.48), channel_id=1, source_target_pairs={{0,130},{2,128},{128,2},{130,0},{1,131},{3,129},{129,3},{131,1},{4... | collective-permute-start | bytes 1572872 | tf_op jit(solution)/shard_map/ppermute | solution.py:33
  32.0 22.8 %collective-permute-start.9 = (bf16[256,1024]{1,0:T(8,128)(2,1)S(1)}, bf16[256,1024]{1,0:T(8,128)(2,1)}, u32[]{:S(2)}, u32[]{:S(2)}) collective-permute-start(bf16[256,1024]{1,0:T(8,128)(2,1)S(1)} %collective-permute-done.7.dg_a), channel_id=1, source_target_pairs={{0,128},{128,0},{1,129},{129,1},{2,130},{130,2},{3,131},{131,3},{4... | collective-permute-start | bytes 1572872 | tf_op jit(solution)/shard_map/ppermute | solution.py:33
  32.1 25.4 %collective-permute-start.10 = (bf16[256,1024]{1,0:T(8,128)(2,1)S(1)}, bf16[256,1024]{1,0:T(8,128)(2,1)}, u32[]{:S(2)}, u32[]{:S(2)}) collective-permute-start(bf16[256,1024]{1,0:T(8,128)(2,1)S(1)} %collective-permute-done.6.xl_b), channel_id=1, source_target_pairs={{0,130},{2,128},{128,2},{130,0},{1,131},{3,129},{129,3},{131,1},{4... | collective-permute-start | bytes 1572872 | tf_op jit(solution)/shard_map/ppermute | solution.py:33
  45.1 20.8 %collective-permute-start.2 = (f32[3,4]{1,0:T(4,128)S(1)}, f32[3,4]{1,0:T(4,128)S(1)}, u32[]{:S(2)}, u32[]{:S(2)}) collective-permute-start(f32[3,4]{1,0:T(4,128)S(1)} %get-tuple-element.69), channel_id=1, source_target_pairs={{0,96},{32,0},{64,32},{96,64},{1,97},{33,1},{65,33},{97,65},{2,98}... | collective-permute-start | bytes 152 | tf_op jit(solution)/shard_map/ppermute | solution.py:33
  48.3 17.7 %collective-permute-start.1 = (f32[3,4]{1,0:T(4,128)S(1)}, f32[3,4]{1,0:T(4,128)S(1)}, u32[]{:S(2)}, u32[]{:S(2)}) collective-permute-start(f32[3,4]{1,0:T(4,128)S(1)} %get-tuple-element.69), channel_id=1, source_target_pairs={{0,64},{32,96},{64,0},{96,32},{1,65},{33,97},{65,1},{97,33},{2,66}... | collective-permute-start | bytes 152 | tf_op jit(solution)/shard_map/ppermute | solution.py:33
  48.3 20.7 %collective-permute-start = (f32[3,4]{1,0:T(4,128)S(1)}, f32[3,4]{1,0:T(4,128)S(1)}, u32[]{:S(2)}, u32[]{:S(2)}) collective-permute-start(f32[3,4]{1,0:T(4,128)S(1)} %get-tuple-element.69), channel_id=1, source_target_pairs={{0,32},{32,64},{64,96},{96,0},{1,33},{33,65},{65,97},{97,1},{2,34}... | collective-permute-start | bytes 152 | tf_op jit(solution)/shard_map/ppermute | solution.py:33
  54.9 33.1 %collective-permute-start.11 = (bf16[512,512]{1,0:T(8,128)(2,1)}, bf16[512,512]{1,0:T(8,128)(2,1)}, u32[]{:S(2)}, u32[]{:S(2)}) collective-permute-start(bf16[512,512]{1,0:T(8,128)(2,1)} %get-tuple-element.47), channel_id=1, source_target_pairs={{0,128},{128,0},{1,129},{129,1},{2,130},{130,2},{3,131},{131,3},{4... | collective-permute-start | bytes 1572872 | tf_op jit(solution)/shard_map/ppermute | solution.py:33
  57.5 27.2 %collective-permute-start.13 = (bf16[512,512]{1,0:T(8,128)(2,1)}, bf16[512,512]{1,0:T(8,128)(2,1)}, u32[]{:S(2)}, u32[]{:S(2)}) collective-permute-start(bf16[512,512]{1,0:T(8,128)(2,1)} %get-tuple-element.47), channel_id=1, source_target_pairs={{0,130},{2,128},{128,2},{130,0},{1,131},{3,129},{129,3},{131,1},{4... | collective-permute-start | bytes 1572872 | tf_op jit(solution)/shard_map/ppermute | solution.py:33
  61.6 17.1 %all-to-all-start.1 = ((bf16[4,64,2048]{2,1,0:T(8,128)(2,1)}), bf16[4,64,2048]{2,1,0:T(8,128)(2,1)S(1)}, u32[]{:S(2)}, u32[]{:S(2)}) async-start(bf16[4,64,2048]{2,1,0:T(8,128)(2,1)} %bitcast.80), calls=%async_computation.1 | async-start | bytes 2097152 | tf_op jit(solution)/shard_map/all_to_all | solution.py:67
  65.9 18.9 %collective-permute-start.12 = (bf16[512,512]{1,0:T(8,128)(2,1)}, bf16[512,512]{1,0:T(8,128)(2,1)}, u32[]{:S(2)}, u32[]{:S(2)}) collective-permute-start(bf16[512,512]{1,0:T(8,128)(2,1)} %get-tuple-element.46), channel_id=1, source_target_pairs={{0,128},{128,0},{1,129},{129,1},{2,130},{130,2},{3,131},{131,3},{4... | collective-permute-start | bytes 1572872 | tf_op jit(solution)/shard_map/ppermute | solution.py:33
  66.0 21.9 %collective-permute-start.14 = (bf16[512,512]{1,0:T(8,128)(2,1)}, bf16[512,512]{1,0:T(8,128)(2,1)}, u32[]{:S(2)}, u32[]{:S(2)}) collective-permute-start(bf16[512,512]{1,0:T(8,128)(2,1)} %get-tuple-element.46), channel_id=1, source_target_pairs={{0,130},{2,128},{128,2},{130,0},{1,131},{3,129},{129,3},{131,1},{4... | collective-permute-start | bytes 1572872 | tf_op jit(solution)/shard_map/ppermute | solution.py:33
  80.7 17.4 %all-to-all-start.2 = ((bf16[4,64,2048]{2,1,0:T(8,128)(2,1)}), bf16[4,64,2048]{2,1,0:T(8,128)(2,1)S(1)}, u32[]{:S(2)}, u32[]{:S(2)}) async-start(bf16[4,64,2048]{2,1,0:T(8,128)(2,1)} %copy-done.13), calls=%async_computation.2 | async-start | bytes 2097152 | tf_op jit(solution)/shard_map/all_to_all | solution.py:67
  107.1 61.8 %collective-permute-start.28 = (bf16[256,512]{1,0:T(8,128)(2,1)}, bf16[256,512]{1,0:T(8,128)(2,1)}, u32[]{:S(2)}, u32[]{:S(2)}) collective-permute-start(bf16[256,512]{1,0:T(8,128)(2,1)} %get-tuple-element.53), channel_id=1, source_target_pairs={{0,130},{2,128},{128,2},{130,0},{1,131},{3,129},{129,3},{131,1},{4... | collective-permute-start | bytes 786440 | tf_op jit(solution)/shard_map/ppermute | solution.py:33
  115.9 16.1 %collective-permute-start.21 = (bf16[72,2048]{1,0:T(8,128)(2,1)}, bf16[72,2048]{1,0:T(8,128)(2,1)S(1)}, u32[]{:S(2)}, u32[]{:S(2)}) collective-permute-start(bf16[72,2048]{1,0:T(8,128)(2,1)} %get-tuple-element.29), channel_id=1, source_target_pairs={{0,64},{32,96},{64,0},{96,32},{1,65},{33,97},{65,1},{97,33},{2,66}... | collective-permute-start | bytes 884744 | tf_op jit(solution)/shard_map/ppermute | solution.py:33
  118.5 18.4 %collective-permute-start.22 = (bf16[72,2048]{1,0:T(8,128)(2,1)}, bf16[72,2048]{1,0:T(8,128)(2,1)S(1)}, u32[]{:S(2)}, u32[]{:S(2)}) collective-permute-start(bf16[72,2048]{1,0:T(8,128)(2,1)} %get-tuple-element.30), channel_id=1, source_target_pairs={{0,96},{32,0},{64,32},{96,64},{1,97},{33,1},{65,33},{97,65},{2,98}... | collective-permute-start | bytes 884744 | tf_op jit(solution)/shard_map/ppermute | solution.py:33
  129.1 40.0 %collective-permute-start.34 = (bf16[256,1024]{1,0:T(8,128)(2,1)}, bf16[256,1024]{1,0:T(8,128)(2,1)}, u32[]{:S(2)}, u32[]{:S(2)}) collective-permute-start(bf16[256,1024]{1,0:T(8,128)(2,1)} %get-tuple-element.43), channel_id=1, source_target_pairs={{0,130},{2,128},{128,2},{130,0},{1,131},{3,129},{129,3},{131,1},{4... | collective-permute-start | bytes 1572872 | tf_op jit(solution)/shard_map/ppermute | solution.py:33
  130.7 42.3 %collective-permute-start.33 = (bf16[256,1024]{1,0:T(8,128)(2,1)}, bf16[256,1024]{1,0:T(8,128)(2,1)}, u32[]{:S(2)}, u32[]{:S(2)}) collective-permute-start(bf16[256,1024]{1,0:T(8,128)(2,1)} %get-tuple-element.43), channel_id=1, source_target_pairs={{0,2},{2,0},{1,3},{3,1},{4,6},{6,4},{5,7},{7,5},{8,10},{10,8},{9,1... | collective-permute-start | bytes 1572872 | tf_op jit(solution)/shard_map/ppermute | solution.py:33
  132.7 42.2 %collective-permute-start.32 = (bf16[256,1024]{1,0:T(8,128)(2,1)}, bf16[256,1024]{1,0:T(8,128)(2,1)}, u32[]{:S(2)}, u32[]{:S(2)}) collective-permute-start(bf16[256,1024]{1,0:T(8,128)(2,1)} %get-tuple-element.42), channel_id=1, source_target_pairs={{0,128},{128,0},{1,129},{129,1},{2,130},{130,2},{3,131},{131,3},{4... | collective-permute-start | bytes 1572872 | tf_op jit(solution)/shard_map/ppermute | solution.py:33
  146.7 16.7 %all-to-all-start.4 = ((bf16[4,64,2048]{2,1,0:T(8,128)(2,1)}), bf16[4,64,2048]{2,1,0:T(8,128)(2,1)S(1)}, u32[]{:S(2)}, u32[]{:S(2)}) async-start(bf16[4,64,2048]{2,1,0:T(8,128)(2,1)} %copy-done.14), calls=%async_computation.4 | async-start | bytes 2097152 | tf_op jit(solution)/shard_map/all_to_all | solution.py:67
  167.9 16.8 %collective-permute-start.37 = (bf16[256,512]{1,0:T(8,128)(2,1)S(1)}, bf16[256,512]{1,0:T(8,128)(2,1)S(1)}, u32[]{:S(2)}, u32[]{:S(2)}) collective-permute-start(bf16[256,512]{1,0:T(8,128)(2,1)S(1)} %copy-done.39), channel_id=1, source_target_pairs={{0,130},{2,128},{128,2},{130,0},{1,131},{3,129},{129,3},{131,1},{4... | collective-permute-start | bytes 786440 | tf_op jit(solution)/shard_map/ppermute | solution.py:33
  169.0 24.6 %collective-permute-start.35 = (bf16[256,512]{1,0:T(8,128)(2,1)S(1)}, bf16[256,512]{1,0:T(8,128)(2,1)}, u32[]{:S(2)}, u32[]{:S(2)}) collective-permute-start(bf16[256,512]{1,0:T(8,128)(2,1)S(1)} %copy-done.39), channel_id=1, source_target_pairs={{0,128},{128,0},{1,129},{129,1},{2,130},{130,2},{3,131},{131,3},{4... | collective-permute-start | bytes 786440 | tf_op jit(solution)/shard_map/ppermute | solution.py:33
  169.1 22.5 %collective-permute-start.36 = (bf16[256,512]{1,0:T(8,128)(2,1)S(1)}, bf16[256,512]{1,0:T(8,128)(2,1)}, u32[]{:S(2)}, u32[]{:S(2)}) collective-permute-start(bf16[256,512]{1,0:T(8,128)(2,1)S(1)} %copy-done.38), channel_id=1, source_target_pairs={{0,2},{2,0},{1,3},{3,1},{4,6},{6,4},{5,7},{7,5},{8,10},{10,8},{9,1... | collective-permute-start | bytes 786440 | tf_op jit(solution)/shard_map/ppermute | solution.py:33
  174.9 50.0 %collective-permute-start.31 = (bf16[256,1024]{1,0:T(8,128)(2,1)S(1)}, bf16[256,1024]{1,0:T(8,128)(2,1)S(1)}, u32[]{:S(2)}, u32[]{:S(2)}) collective-permute-start(bf16[256,1024]{1,0:T(8,128)(2,1)S(1)} %get-tuple-element.45), channel_id=1, source_target_pairs={{0,130},{2,128},{128,2},{130,0},{1,131},{3,129},{129,3},{131,1},{4... | collective-permute-start | bytes 1572872 | tf_op jit(solution)/shard_map/ppermute | solution.py:33
  184.7 40.2 %collective-permute-start.30 = (bf16[256,1024]{1,0:T(8,128)(2,1)S(1)}, bf16[256,1024]{1,0:T(8,128)(2,1)S(1)}, u32[]{:S(2)}, u32[]{:S(2)}) collective-permute-start(bf16[256,1024]{1,0:T(8,128)(2,1)S(1)} %get-tuple-element.45), channel_id=1, source_target_pairs={{0,2},{2,0},{1,3},{3,1},{4,6},{6,4},{5,7},{7,5},{8,10},{10,8},{9,1... | collective-permute-start | bytes 1572872 | tf_op jit(solution)/shard_map/ppermute | solution.py:33
  184.7 40.2 %collective-permute-start.29 = (bf16[256,1024]{1,0:T(8,128)(2,1)S(1)}, bf16[256,1024]{1,0:T(8,128)(2,1)}, u32[]{:S(2)}, u32[]{:S(2)}) collective-permute-start(bf16[256,1024]{1,0:T(8,128)(2,1)S(1)} %get-tuple-element.44), channel_id=1, source_target_pairs={{0,128},{128,0},{1,129},{129,1},{2,130},{130,2},{3,131},{131,3},{4... | collective-permute-start | bytes 1572872 | tf_op jit(solution)/shard_map/ppermute | solution.py:33
  185.5 15.8 %all-to-all-start.5 = ((bf16[8,128,128]{2,1,0:T(8,128)(2,1)}), bf16[8,128,128]{2,1,0:T(8,128)(2,1)S(1)}, u32[]{:S(2)}, u32[]{:S(2)}) async-start(bf16[8,128,128]{2,1,0:T(8,128)(2,1)} %bitcast.28), calls=%async_computation.5 | async-start | bytes 524288 | tf_op jit(solution)/shard_map/all_to_all | solution.py:67
  191.5 33.3 %collective-permute-start.26 = (bf16[256,512]{1,0:T(8,128)(2,1)}, bf16[256,512]{1,0:T(8,128)(2,1)S(1)}, u32[]{:S(2)}, u32[]{:S(2)}) collective-permute-start(bf16[256,512]{1,0:T(8,128)(2,1)} %get-tuple-element.53), channel_id=1, source_target_pairs={{0,128},{128,0},{1,129},{129,1},{2,130},{130,2},{3,131},{131,3},{4... | collective-permute-start | bytes 786440 | tf_op jit(solution)/shard_map/ppermute | solution.py:33
  193.6 29.4 %collective-permute-start.27 = (bf16[256,512]{1,0:T(8,128)(2,1)S(1)}, bf16[256,512]{1,0:T(8,128)(2,1)S(1)}, u32[]{:S(2)}, u32[]{:S(2)}) collective-permute-start(bf16[256,512]{1,0:T(8,128)(2,1)S(1)} %copy-done.37), channel_id=1, source_target_pairs={{0,2},{2,0},{1,3},{3,1},{4,6},{6,4},{5,7},{7,5},{8,10},{10,8},{9,1... | collective-permute-start | bytes 786440 | tf_op jit(solution)/shard_map/ppermute | solution.py:33
  (57 other events, 520.4 us)

commit v3 on v2

--- a/solution.py
+++ b/solution.py
@@ -237,11 +237,10 @@
     return jnp.transpose(jnp.broadcast_to(row, (128, row.shape[1])))
 
 
-def combine_kernel(hidden_ref, stay_ref, got_ref, vec_ref, full_ref, half_ref, sums_ref):
+def combine_kernel(hidden_ref, stay_ref, got_ref, vec_ref, half_ref, sums_ref):
     squares = products = 0.0
     for i in range(2):
         combined = hidden_ref[i].astype(F32) + stay_ref[i] + got_ref[i].astype(F32)
-        full_ref[i] = combined
         half_ref[i] = combined.astype(BF16)
         squares += jnp.sum(combined * combined, axis=1, keepdims=True)
         products += jnp.sum(combined * vec_ref[i : i + 1], axis=1, keepdims=True)
@@ -252,9 +251,9 @@
 def combine(hidden, stay, got, vec):
     return pl.pallas_call(
         combine_kernel,
-        out_shape=(like(stay.shape, F32), like(stay.shape, BF16), like((2, stay.shape[1]), F32)),
+        out_shape=(like(stay.shape, BF16), like((2, stay.shape[1]), F32)),
         in_specs=[VMEM] * 4,
-        out_specs=(VMEM,) * 3,
+        out_specs=(VMEM,) * 2,
         name="combine",
         compiler_params=limit(6),
     )(hidden, stay, got, vec)
@@ -319,9 +318,9 @@
     )(place, own, partner, vec, *blocks)
 
 
-def back_kernel(
-    place_ref, weight_ref, every_ref, pooler_ref, gate_ref, part_0, part_1, part_2, part_3,
-    copies_ref, by_vec_ref, by_combined_ref, penalized_ref, *, features,
+def token_kernel(
+    place_ref, weight_ref, every_ref, pooler_ref,
+    by_vec_ref, by_combined_ref, piece_vec_ref, piece_combined_ref, penalized_ref, *, features,
 ):
     members, rows = every_ref.shape[1], every_ref.shape[3]
     heads = lax.broadcasted_iota(jnp.int32, (members, 1), 0)
@@ -356,40 +355,24 @@
         by_vec_ref[at] = as_columns(tok_weight * inverse)
         by_combined_ref[at] = as_columns(tok_weight * scores * inverse * inverse / features)
     penalized_ref[...] = penalized
-    piece = gate_ref.shape[0]
+    piece = piece_vec_ref.shape[0]
     start = pl.multiple_of(place_ref[0] * piece, piece)
-    by_vec = by_vec_ref[pl.ds(start, piece), 0:1]
-    by_combined = by_combined_ref[pl.ds(start, piece), 0:1]
-    parts = (part_0, part_1, part_2, part_3)
-    step = 512
-    for at in range(0, gate_ref.shape[1], step):
-        cols = slice(at, at + step)
-        combined_out = sum(part[:piece, cols].astype(F32) for part in parts)
-        vec_out = jnp.sum(
-            sum(part[piece:, cols].astype(F32) for part in parts), axis=0, keepdims=True
-        )
-        raw = by_vec * vec_out - by_combined * combined_out
-        back = (raw * silu_slope(gate_ref[:, cols])).astype(BF16)
-        for k in range(copies_ref.shape[0]):
-            copies_ref[k, :, cols] = back
-
-
-def back_of(place, weight, every, pooler, gate, parts, features):
-    piece, width = gate.shape
+    piece_vec_ref[...] = by_vec_ref[pl.ds(start, piece), :]
+    piece_combined_ref[...] = by_combined_ref[pl.ds(start, piece), :]
+
+
+def token_factors(place, weight, every, pooler, piece, features):
     rows = every.shape[3]
     return pl.pallas_call(
-        functools.partial(back_kernel, features=features),
-        out_shape=(
-            like((4, piece, width), BF16),
-            like((2 * rows, 128), F32),
-            like((2 * rows, 128), F32),
-            like((1, 128), F32),
-        ),
-        in_specs=[SMEM, SMEM] + [VMEM] * 7,
-        out_specs=(VMEM,) * 4,
-        name="back",
-        compiler_params=limit(8),
-    )(place, weight, every, pooler, gate, *parts)
+        functools.partial(token_kernel, features=features),
+        out_shape=(like((2 * rows, 128), F32),) * 2
+        + (like((piece, 128), F32),) * 2
+        + (like((1, 128), F32),),
+        in_specs=[SMEM, SMEM, VMEM, VMEM],
+        out_specs=(VMEM,) * 5,
+        name="tokens",
+        compiler_params=limit(4),
+    )(place, weight, every, pooler)
 
 
 def local(hidden, w_in, w_out, score_vec, lengths, reward_offset, seq_weight):
@@ -432,7 +415,7 @@
         ]
     )
     away, stay = branch_of(activated, v_blocks)
-    combined, combined_half, sums = combine(slab_mine, stay, over_cores(away), vec)
+    combined_half, sums = combine(slab_mine, stay, over_cores(away), vec)
     combined_partner = over_cores(combined_half)
     place = jnp.stack([y, z]).astype(jnp.int32)
     parts = against_out(place, combined_half, combined_partner, vec, v_blocks)
@@ -442,10 +425,13 @@
     ]
     sums = jnp.concatenate([sums, over_cores(sums)])
     every = sent_to_all(sums, ("y", "z")).reshape(SIZES[1], members, 4, rows)
-    copies, by_vec, by_combined, penalized = back_of(
-        place, weight, every, pooler, gate, parts, features
-    )
-    by_vec, by_combined = by_vec[:, :1], by_combined[:, :1]
+    piece = gate.shape[0]
+    *factors, penalized = token_factors(place, weight, every, pooler, piece, features)
+    by_vec, by_combined, piece_vec, piece_combined = (factor[:, :1] for factor in factors)
+    of_y = sum(part.astype(F32) for part in parts)
+    vec_out = jnp.sum(of_y[piece:], axis=0, keepdims=True)
+    back_raw = piece_vec * vec_out - piece_combined * of_y[:piece]
+    back_piece = (back_raw * silu_slope(gate)).astype(BF16)
     combined_both = jnp.concatenate([combined_half, combined_partner], axis=1)
     slopes = (by_vec * vec[:, None] - by_combined * combined_both.astype(F32)).astype(BF16)
 
@@ -453,14 +439,14 @@
         return (own, over_xl(by_xl), over_xh(by_xh), over_diagonal(by_diagonal))
 
     act_all = quarters(act_o, act_o, act_t, act_t)
-    back_gate = gathered_over_y(copies)
+    back_gate = sent_to_all(back_piece, "y").reshape(2 * rows, -1)
     slope_all = quarters(slopes[0], slopes[1], slopes[0], slopes[1])
     hid_o, hid_t = jnp.concatenate([slab_mine, slab_partner], axis=1)
     hid_all = quarters(hid_o, hid_t, hid_o, hid_t)
     back_o, back_t = back_gate[:, :units], back_gate[:, units:]
     back_all = quarters(back_o, back_o, back_t, back_t)
     away, stay = back_hidden(back_gate, w_blocks)
-    direct = by_vec[:rows] * vec[:, None] - by_combined[:rows] * combined
+    direct = by_vec[:rows] * vec[:, None] - by_combined[:rows] * combined_half.astype(F32)
     term = direct + stay + over_cores(away).astype(F32)
     parts = jnp.moveaxis(term.astype(BF16).reshape(2, rows, 4, -1), 2, 1).reshape(8, rows, -1)
     from_heads = exchanged(parts, "z")

time: 240 us -> 252 us (1.050)
  the two profiles are of different devices: /device:TPU:70 before, /device:TPU:7 now
where the time goes in v3:
time: 252 us; the launch traced here: 248 us
  waiting for transfers between devices  105 us (42%)
  starting transfers between devices  91.2 us (36%)
  local copies, waits for them, and re-layouts  23.4 us (9%)
  Pallas kernels  13.3 us (5%)
  matrix products  8.14 us (3%)
  other arithmetic  4.97 us (2%)
    ppermute x38, waiting for transfers between devices, permuted(): return lax.ppermute(array, axes, pairs)  75.5 us
    ppermute x38, starting transfers between devices, permuted(): return lax.ppermute(array, axes, pairs)  63.1 us
    all_to_all x6, waiting for transfers between devices, exchanged(): return lax.all_to_all(array, axes, 0, 0, tiled=True)  29.7 us
    all_to_all x6, starting transfers between devices, exchanged(): return lax.all_to_all(array, axes, 0, 0, tiled=True)  28.1 us
    unnamed x70, local copies, waits for them, and re-layouts  11.4 us
    dot_general x2, matrix products, t_mul(): lax.dot_general(left, right, (((0,), (0,)), ((), ())), preferred_element_...  8.14 us
  transfers between devices with their start and end apart: 44, of which 19 were waited for; matrix products, arithmetic and copies ran while one was open for 9% of the time, Pallas kernels for 4%

profile of v3, /device:TPU:7, one launch (start us, length us, event | category | flops | bytes accessed | tf_op | source)
XLA Modules:
  0.0 247.5 jit_solution(15844556754460595119)
XLA Ops:
  3.8 11.4 %collective-permute-start.3 = (bf16[128,128]{1,0:T(8,128)(2,1)S(1)}, bf16[128,128]{1,0:T(8,128)(2,1)S(1)}, u32[]{:S(2)}, u32[]{:S(2)}) collective-permute-start(bf16[128,128]{1,0:T(8,128)(2,1)S(1)} %copy-done.31), channel_id=1, source_target_pairs={{0,0},{1,4},{2,8},{3,12},{4,32},{5,36},{6,40},{7,44},{8,64},{9,68}... | collective-permute-start | bytes 98312 | tf_op jit(solution)/shard_map/ppermute | solution.py:33
  15.2 5.7 %collective-permute-done.3 = bf16[128,128]{1,0:T(8,128)(2,1)S(1)} collective-permute-done((bf16[128,128]{1,0:T(8,128)(2,1)S(1)}, bf16[128,128]{1,0:T(8,128)(2,1)S(1)}, u32[]{:S(2)}, u32[]{:S(2)}) %collective-permute-start.3) | collective-permute-done | bytes 32800 | tf_op jit(solution)/shard_map/ppermute | solution.py:33
  21.6 4.9 %all-to-all-start = ((bf16[8,128,128]{2,1,0:T(8,128)(2,1)}), bf16[8,128,128]{2,1,0:T(8,128)(2,1)S(1)}, u32[]{:S(2)}, u32[]{:S(2)}) async-start(bf16[8,128,128]{2,1,0:T(8,128)(2,1)} %broadcast_in_dim.10), calls=%async_computation | async-start | bytes 524288 | tf_op jit(solution)/shard_map/all_to_all | solution.py:67
  26.5 5.2 %collective-permute-start.5 = (bf16[256,1024]{1,0:T(8,128)(2,1)}, bf16[256,1024]{1,0:T(8,128)(2,1)}, u32[]{:S(2)}, u32[]{:S(2)}) collective-permute-start(bf16[256,1024]{1,0:T(8,128)(2,1)} %get-tuple-element.49), channel_id=1, source_target_pairs={{0,128},{128,0},{1,129},{129,1},{2,130},{130,2},{3,131},{131,3},{4... | collective-permute-start | bytes 1572872 | tf_op jit(solution)/shard_map/ppermute | solution.py:33
  32.0 2.6 %collective-permute-start.10 = (bf16[256,1024]{1,0:T(8,128)(2,1)S(1)}, bf16[256,1024]{1,0:T(8,128)(2,1)}, u32[]{:S(2)}, u32[]{:S(2)}) collective-permute-start(bf16[256,1024]{1,0:T(8,128)(2,1)S(1)} %collective-permute-done.6.xl_b), channel_id=1, source_target_pairs={{0,130},{2,128},{128,2},{130,0},{1,131},{3,129},{129,3},{131,1},{4... | collective-permute-start | bytes 1572872 | tf_op jit(solution)/shard_map/ppermute | solution.py:33
  37.8 3.4 %collective-permute-start.4 = (bf16[2,128,512]{2,1,0:T(8,128)(2,1)S(1)}, bf16[2,128,512]{2,1,0:T(8,128)(2,1)S(1)}, u32[]{:S(2)}, u32[]{:S(2)}) collective-permute-start(bf16[2,128,512]{2,1,0:T(8,128)(2,1)S(1)} %bitcast.81), channel_id=1, source_target_pairs={{0,1},{1,0},{2,3},{3,2},{4,5},{5,4},{6,7},{7,6},{8,9},{9,8},{10,11... | collective-permute-start | bytes 786440 | tf_op jit(solution)/shard_map/ppermute | solution.py:33
  45.5 9.0 %collective-permute-done.9.xh_a = bf16[256,1024]{1,0:T(8,128)(2,1)} collective-permute-done((bf16[256,1024]{1,0:T(8,128)(2,1)S(1)}, bf16[256,1024]{1,0:T(8,128)(2,1)}, u32[]{:S(2)}, u32[]{:S(2)}) %collective-permute-start.9) | collective-permute-done | bytes 524320 | tf_op jit(solution)/shard_map/ppermute | solution.py:33
  57.0 2.8 %gate.1 = bf16[256,2048]{1,0:T(8,128)(2,1)S(1)} custom-call(bf16[2,128,512]{2,1,0:T(8,128)(2,1)S(1)} %bitcast.82, bf16[2,128,512]{2,1,0:T(8,128)(2,1)S(1)} %collective-permute-done.4.partner_ref, bf16[512,1024]{1,0:T(8,128)(2,1)S(1)} %bitcast.78, bf16[256,1024]{1,0:T(8,128)(2,1)} %collective-permute-done.5.xl_a, ...), custom_call_target="tpu_custom_call" | custom-call | tf_op jit(solution)/shard_map/gate/pallas_call | solution.py:164
  60.7 3.5 %all-to-all-start.1 = ((bf16[4,64,2048]{2,1,0:T(8,128)(2,1)}), bf16[4,64,2048]{2,1,0:T(8,128)(2,1)S(1)}, u32[]{:S(2)}, u32[]{:S(2)}) async-start(bf16[4,64,2048]{2,1,0:T(8,128)(2,1)} %bitcast.80), calls=%async_computation.1 | async-start | bytes 2097152 | tf_op jit(solution)/shard_map/all_to_all | solution.py:67
  64.4 2.5 %collective-permute-start.14 = (bf16[512,512]{1,0:T(8,128)(2,1)}, bf16[512,512]{1,0:T(8,128)(2,1)}, u32[]{:S(2)}, u32[]{:S(2)}) collective-permute-start(bf16[512,512]{1,0:T(8,128)(2,1)} %get-tuple-element.46), channel_id=1, source_target_pairs={{0,130},{2,128},{128,2},{130,0},{1,131},{3,129},{129,3},{131,1},{4... | collective-permute-start | bytes 1572872 | tf_op jit(solution)/shard_map/ppermute | solution.py:33
  67.0 10.3 %all-to-all-done.1.parts_ref = bf16[4,64,2048]{2,1,0:T(8,128)(2,1)S(1)} async-done(((bf16[4,64,2048]{2,1,0:T(8,128)(2,1)}), bf16[4,64,2048]{2,1,0:T(8,128)(2,1)S(1)}, u32[]{:S(2)}, u32[]{:S(2)}) %all-to-all-start.1) | async-done | bytes 1048608 | tf_op jit(solution)/shard_map/all_to_all | solution.py:67
  79.2 3.5 %all-to-all-start.2 = ((bf16[4,64,2048]{2,1,0:T(8,128)(2,1)}), bf16[4,64,2048]{2,1,0:T(8,128)(2,1)S(1)}, u32[]{:S(2)}, u32[]{:S(2)}) async-start(bf16[4,64,2048]{2,1,0:T(8,128)(2,1)} %copy-done.15), calls=%async_computation.2 | async-start | bytes 2097152 | tf_op jit(solution)/shard_map/all_to_all | solution.py:67
  85.7 8.4 %collective-permute-done.15.xh_a = bf16[512,512]{1,0:T(8,128)(2,1)S(1)} collective-permute-done((bf16[512,512]{1,0:T(8,128)(2,1)}, bf16[512,512]{1,0:T(8,128)(2,1)S(1)}, u32[]{:S(2)}, u32[]{:S(2)}) %collective-permute-start.15) | collective-permute-done | bytes 524320 | tf_op jit(solution)/shard_map/ppermute | solution.py:33
  98.5 2.8 %branch.1 = (bf16[2,128,512]{2,1,0:T(8,128)(2,1)S(1)}, f32[2,128,512]{2,1,0:T(8,128)S(1)}) custom-call(bf16[256,2048]{1,0:T(8,128)(2,1)S(1)} %bitcast.72, bf16[1024,512]{1,0:T(8,128)(2,1)S(1)} %bitcast.76, bf16[512,512]{1,0:T(8,128)(2,1)} %collective-permute-done.11.xl_a, bf16[512,512]{1,0:T(8,128)(2,1)} %collective-permute-done.12.xl_b, ...), custom_call_target="tpu_custom_call" | custom-call | tf_op jit(solution)/shard_map/branch/pallas_call | solution.py:195
  101.3 4.0 %collective-permute-start.17 = (bf16[2,128,512]{2,1,0:T(8,128)(2,1)S(1)}, bf16[2,128,512]{2,1,0:T(8,128)(2,1)S(1)}, u32[]{:S(2)}, u32[]{:S(2)}) collective-permute-start(bf16[2,128,512]{2,1,0:T(8,128)(2,1)S(1)} %get-tuple-element.23), channel_id=1, source_target_pairs={{0,1},{1,0},{2,3},{3,2},{4,5},{5,4},{6,7},{7,6},{8,9},{9,8},{10,11... | collective-permute-start | bytes 786440 | tf_op jit(solution)/shard_map/ppermute | solution.py:33
  111.4 9.1 %all-to-all-start.3 = ((f32[32,4,128]{2,1,0:T(4,128)}), f32[32,4,128]{2,1,0:T(4,128)S(1)}, u32[]{:S(2)}, u32[]{:S(2)}) async-start(f32[32,4,128]{2,1,0:T(4,128)} %broadcast_in_dim.11), calls=%async_computation.3 | async-start | bytes 131072 | tf_op jit(solution)/shard_map/all_to_all | solution.py:67
  122.2 7.2 %all-to-all-done.3 = f32[32,4,128]{2,1,0:T(4,128)S(1)} async-done(((f32[32,4,128]{2,1,0:T(4,128)}), f32[32,4,128]{2,1,0:T(4,128)S(1)}, u32[]{:S(2)}, u32[]{:S(2)}) %all-to-all-start.3) | async-done | bytes 65568 | tf_op jit(solution)/shard_map/all_to_all | solution.py:67
  133.9 3.1 %against_out.1 = (bf16[72,2048]{1,0:T(8,128)(2,1)S(1)}, bf16[72,2048]{1,0:T(8,128)(2,1)S(1)}, bf16[72,2048]{1,0:T(8,128)(2,1)S(1)}, bf16[72,2048]{1,0:T(8,128)(2,1)S(1)}) custom-call(s32[2]{0:T(128)S(1)} %pad_add_fusion.place_ref, bf16[2,128,512]{2,1,0:T(8,128)(2,1)} %get-tuple-element.28.own_ref, ...), custom_call_target="tpu_custom_call" | custom-call | tf_op jit(solution)/shard_map/against_out/pallas_call | solution.py:307
  139.6 4.5 %collective-permute-done.23 = bf16[72,2048]{1,0:T(8,128)(2,1)S(1)} collective-permute-done((bf16[72,2048]{1,0:T(8,128)(2,1)S(1)}, bf16[72,2048]{1,0:T(8,128)(2,1)S(1)}, u32[]{:S(2)}, u32[]{:S(2)}) %collective-permute-start.23) | collective-permute-done | bytes 294944 | tf_op jit(solution)/shard_map/ppermute | solution.py:33
  146.3 8.5 %collective-permute-done.21 = bf16[72,2048]{1,0:T(8,128)(2,1)S(1)} collective-permute-done((bf16[72,2048]{1,0:T(8,128)(2,1)S(1)}, bf16[72,2048]{1,0:T(8,128)(2,1)S(1)}, u32[]{:S(2)}, u32[]{:S(2)}) %collective-permute-start.21) | collective-permute-done | bytes 294944 | tf_op jit(solution)/shard_map/ppermute | solution.py:33
  156.4 3.6 %all-to-all-start.4 = ((bf16[4,64,2048]{2,1,0:T(8,128)(2,1)}), bf16[4,64,2048]{2,1,0:T(8,128)(2,1)S(1)}, u32[]{:S(2)}, u32[]{:S(2)}) async-start(bf16[4,64,2048]{2,1,0:T(8,128)(2,1)} %broadcast_in_dim.12), calls=%async_computation.4 | async-start | bytes 2097152 | tf_op jit(solution)/shard_map/all_to_all | solution.py:67
  163.3 11.5 %all-to-all-done.4 = bf16[4,64,2048]{2,1,0:T(8,128)(2,1)S(1)} async-done(((bf16[4,64,2048]{2,1,0:T(8,128)(2,1)}), bf16[4,64,2048]{2,1,0:T(8,128)(2,1)S(1)}, u32[]{:S(2)}, u32[]{:S(2)}) %all-to-all-start.4) | async-done | bytes 1048608 | tf_op jit(solution)/shard_map/all_to_all | solution.py:67
  174.8 2.8 %back_hidden.1 = (bf16[2,128,512]{2,1,0:T(8,128)(2,1)S(1)}, f32[2,128,512]{2,1,0:T(8,128)S(1)}) custom-call(bf16[256,2048]{1,0:T(8,128)(2,1)S(1)} %bitcast.74, bf16[512,1024]{1,0:T(8,128)(2,1)S(1)} %bitcast.79, bf16[256,1024]{1,0:T(8,128)(2,1)} %collective-permute-done.5.xl_a, bf16[256,1024]{1,0:T(8,128)(2,1)S(1)} %copy-done.6, ...), custom_call_target="tpu_custom_call" | custom-call | tf_op jit(solution)/shard_map/back_hidden/pallas_call | solution.py:222
  181.9 3.5 %collective-permute-start.19 = (f32[1,4]{1,0:T(1,128)S(1)}, f32[1,4]{1,0:T(1,128)S(1)}, u32[]{:S(2)}, u32[]{:S(2)}) collective-permute-start(f32[1,4]{1,0:T(1,128)S(1)} %bitcast.85), channel_id=1, source_target_pairs={{0,0},{1,32},{2,64},{3,96},{32,1},{33,33},{34,65},{35,97},{64,2},{... | collective-permute-start | bytes 56 | tf_op jit(solution)/shard_map/ppermute | solution.py:33
  185.4 5.0 %collective-permute-done.19 = f32[1,4]{1,0:T(1,128)S(1)} collective-permute-done((f32[1,4]{1,0:T(1,128)S(1)}, f32[1,4]{1,0:T(1,128)S(1)}, u32[]{:S(2)}, u32[]{:S(2)}) %collective-permute-start.19) | collective-permute-done | bytes 48 | tf_op jit(solution)/shard_map/ppermute | solution.py:33
  190.6 3.8 %collective-permute-start.31 = (bf16[256,1024]{1,0:T(8,128)(2,1)S(1)}, bf16[256,1024]{1,0:T(8,128)(2,1)S(1)}, u32[]{:S(2)}, u32[]{:S(2)}) collective-permute-start(bf16[256,1024]{1,0:T(8,128)(2,1)S(1)} %get-tuple-element.45), channel_id=1, source_target_pairs={{0,130},{2,128},{128,2},{130,0},{1,131},{3,129},{129,3},{131,1},{4... | collective-permute-start | bytes 1572872 | tf_op jit(solution)/shard_map/ppermute | solution.py:33
  195.8 3.4 %all-to-all-start.5 = ((bf16[8,128,128]{2,1,0:T(8,128)(2,1)}), bf16[8,128,128]{2,1,0:T(8,128)(2,1)S(1)}, u32[]{:S(2)}, u32[]{:S(2)}) async-start(bf16[8,128,128]{2,1,0:T(8,128)(2,1)} %bitcast.28), calls=%async_computation.5 | async-start | bytes 524288 | tf_op jit(solution)/shard_map/all_to_all | solution.py:67
  201.7 4.4 %collective-permute-start.27 = (bf16[256,512]{1,0:T(8,128)(2,1)S(1)}, bf16[256,512]{1,0:T(8,128)(2,1)S(1)}, u32[]{:S(2)}, u32[]{:S(2)}) collective-permute-start(bf16[256,512]{1,0:T(8,128)(2,1)S(1)} %copy-done.27), channel_id=1, source_target_pairs={{0,2},{2,0},{1,3},{3,1},{4,6},{6,4},{5,7},{7,5},{8,10},{10,8},{9,1... | collective-permute-start | bytes 786440 | tf_op jit(solution)/shard_map/ppermute | solution.py:33
  206.1 4.2 %fusion.16 = f32[1,1024,512]{2,1,0:T(8,128)} fusion(bf16[256,1024]{1,0:T(8,128)(2,1)} %collective-permute-done.34, bf16[256,1024]{1,0:T(8,128)(2,1)} %collective-permute-done.33, bf16[256,1024]{1,0:T(8,128)(2,1)} %collective-permute-done.32, bf16[256,1024]{1,0:T(8,128)(2,1)} %get-tuple-element.42, bf16[256,512]{1,0:T(8,128)(2,1)S(1)} %collective-permute-done.37, ...), kind=kOutput, calls=%fused_computation.16 | convolution fusion | flops 1086324736 | bytes 5242880 | tf_op jit(solution)/shard_map/dot_general | solution.py:96
  210.3 23.9 %collective-permute-done.27 = bf16[256,512]{1,0:T(8,128)(2,1)S(1)} collective-permute-done((bf16[256,512]{1,0:T(8,128)(2,1)S(1)}, bf16[256,512]{1,0:T(8,128)(2,1)S(1)}, u32[]{:S(2)}, u32[]{:S(2)}) %collective-permute-start.27) | collective-permute-done | bytes 262176 | tf_op jit(solution)/shard_map/ppermute | solution.py:33
  234.2 8.2 %collective-permute-start.25 = (bf16[128,128]{1,0:T(8,128)(2,1)S(1)}, bf16[128,128]{1,0:T(8,128)(2,1)S(1)}, u32[]{:S(2)}, u32[]{:S(2)}) collective-permute-start(bf16[128,128]{1,0:T(8,128)(2,1)S(1)} %reduce_sum.22), channel_id=1, source_target_pairs={{0,0},{1,32},{2,64},{3,96},{4,1},{5,33},{6,65},{7,97},{8,2},{9,34}... | collective-permute-start | bytes 98312 | tf_op jit(solution)/shard_map/ppermute | solution.py:33
  242.4 4.0 %fusion.19 = f32[1,512,1024]{2,1,0:T(8,128)} fusion(bf16[256,1024]{1,0:T(8,128)(2,1)S(1)} %collective-permute-done.31, bf16[256,1024]{1,0:T(8,128)(2,1)} %collective-permute-done.30, bf16[256,1024]{1,0:T(8,128)(2,1)} %collective-permute-done.29, bf16[256,1024]{1,0:T(8,128)(2,1)S(1)} %get-tuple-element.44, bf16[256,512]{1,0:T(8,128)(2,1)} %collective-permute-done.28, ...), kind=kOutput, calls=%fused_computation.17 | convolution fusion | flops 1086324736 | bytes 5242880 | tf_op jit(solution)/shard_map/dot_general | solution.py:96
  (179 shorter events, 55.6 us)
Async XLA Ops:
  3.0 28.7 %collective-permute-start.7 = (bf16[256,1024]{1,0:T(8,128)(2,1)}, bf16[256,1024]{1,0:T(8,128)(2,1)S(1)}, u32[]{:S(2)}, u32[]{:S(2)}) collective-permute-start(bf16[256,1024]{1,0:T(8,128)(2,1)} %get-tuple-element.49), channel_id=1, source_target_pairs={{0,130},{2,128},{128,2},{130,0},{1,131},{3,129},{129,3},{131,1},{4... | collective-permute-start | bytes 1572872 | tf_op jit(solution)/shard_map/ppermute | solution.py:33
  3.0 28.9 %collective-permute-start.6 = (bf16[256,1024]{1,0:T(8,128)(2,1)}, bf16[256,1024]{1,0:T(8,128)(2,1)S(1)}, u32[]{:S(2)}, u32[]{:S(2)}) collective-permute-start(bf16[256,1024]{1,0:T(8,128)(2,1)} %get-tuple-element.48), channel_id=1, source_target_pairs={{0,128},{128,0},{1,129},{129,1},{2,130},{130,2},{3,131},{131,3},{4... | collective-permute-start | bytes 1572872 | tf_op jit(solution)/shard_map/ppermute | solution.py:33
  3.8 17.0 %collective-permute-start.3 = (bf16[128,128]{1,0:T(8,128)(2,1)S(1)}, bf16[128,128]{1,0:T(8,128)(2,1)S(1)}, u32[]{:S(2)}, u32[]{:S(2)}) collective-permute-start(bf16[128,128]{1,0:T(8,128)(2,1)S(1)} %copy-done.31), channel_id=1, source_target_pairs={{0,0},{1,4},{2,8},{3,12},{4,32},{5,36},{6,40},{7,44},{8,64},{9,68}... | collective-permute-start | bytes 98312 | tf_op jit(solution)/shard_map/ppermute | solution.py:33
  21.6 14.4 %all-to-all-start = ((bf16[8,128,128]{2,1,0:T(8,128)(2,1)}), bf16[8,128,128]{2,1,0:T(8,128)(2,1)S(1)}, u32[]{:S(2)}, u32[]{:S(2)}) async-start(bf16[8,128,128]{2,1,0:T(8,128)(2,1)} %broadcast_in_dim.10), calls=%async_computation | async-start | bytes 524288 | tf_op jit(solution)/shard_map/all_to_all | solution.py:67
  26.5 16.8 %collective-permute-start.5 = (bf16[256,1024]{1,0:T(8,128)(2,1)}, bf16[256,1024]{1,0:T(8,128)(2,1)}, u32[]{:S(2)}, u32[]{:S(2)}) collective-permute-start(bf16[256,1024]{1,0:T(8,128)(2,1)} %get-tuple-element.49), channel_id=1, source_target_pairs={{0,128},{128,0},{1,129},{129,1},{2,130},{130,2},{3,131},{131,3},{4... | collective-permute-start | bytes 1572872 | tf_op jit(solution)/shard_map/ppermute | solution.py:33
  31.7 13.7 %collective-permute-start.8 = (bf16[256,1024]{1,0:T(8,128)(2,1)}, bf16[256,1024]{1,0:T(8,128)(2,1)}, u32[]{:S(2)}, u32[]{:S(2)}) collective-permute-start(bf16[256,1024]{1,0:T(8,128)(2,1)} %get-tuple-element.48), channel_id=1, source_target_pairs={{0,130},{2,128},{128,2},{130,0},{1,131},{3,129},{129,3},{131,1},{4... | collective-permute-start | bytes 1572872 | tf_op jit(solution)/shard_map/ppermute | solution.py:33
  31.7 22.8 %collective-permute-start.9 = (bf16[256,1024]{1,0:T(8,128)(2,1)S(1)}, bf16[256,1024]{1,0:T(8,128)(2,1)}, u32[]{:S(2)}, u32[]{:S(2)}) collective-permute-start(bf16[256,1024]{1,0:T(8,128)(2,1)S(1)} %collective-permute-done.7.dg_a), channel_id=1, source_target_pairs={{0,128},{128,0},{1,129},{129,1},{2,130},{130,2},{3,131},{131,3},{4... | collective-permute-start | bytes 1572872 | tf_op jit(solution)/shard_map/ppermute | solution.py:33
  32.0 24.7 %collective-permute-start.10 = (bf16[256,1024]{1,0:T(8,128)(2,1)S(1)}, bf16[256,1024]{1,0:T(8,128)(2,1)}, u32[]{:S(2)}, u32[]{:S(2)}) collective-permute-start(bf16[256,1024]{1,0:T(8,128)(2,1)S(1)} %collective-permute-done.6.xl_b), channel_id=1, source_target_pairs={{0,130},{2,128},{128,2},{130,0},{1,131},{3,129},{129,3},{131,1},{4... | collective-permute-start | bytes 1572872 | tf_op jit(solution)/shard_map/ppermute | solution.py:33
  43.3 21.0 %collective-permute-start.2 = (f32[3,4]{1,0:T(4,128)S(1)}, f32[3,4]{1,0:T(4,128)S(1)}, u32[]{:S(2)}, u32[]{:S(2)}) collective-permute-start(f32[3,4]{1,0:T(4,128)S(1)} %get-tuple-element.69), channel_id=1, source_target_pairs={{0,96},{32,0},{64,32},{96,64},{1,97},{33,1},{65,33},{97,65},{2,98}... | collective-permute-start | bytes 152 | tf_op jit(solution)/shard_map/ppermute | solution.py:33
  45.4 19.0 %collective-permute-start.1 = (f32[3,4]{1,0:T(4,128)S(1)}, f32[3,4]{1,0:T(4,128)S(1)}, u32[]{:S(2)}, u32[]{:S(2)}) collective-permute-start(f32[3,4]{1,0:T(4,128)S(1)} %get-tuple-element.69), channel_id=1, source_target_pairs={{0,64},{32,96},{64,0},{96,32},{1,65},{33,97},{65,1},{97,33},{2,66}... | collective-permute-start | bytes 152 | tf_op jit(solution)/shard_map/ppermute | solution.py:33
  45.4 21.5 %collective-permute-start = (f32[3,4]{1,0:T(4,128)S(1)}, f32[3,4]{1,0:T(4,128)S(1)}, u32[]{:S(2)}, u32[]{:S(2)}) collective-permute-start(f32[3,4]{1,0:T(4,128)S(1)} %get-tuple-element.69), channel_id=1, source_target_pairs={{0,32},{32,64},{64,96},{96,0},{1,33},{33,65},{65,97},{97,1},{2,34}... | collective-permute-start | bytes 152 | tf_op jit(solution)/shard_map/ppermute | solution.py:33
  54.6 31.1 %collective-permute-start.11 = (bf16[512,512]{1,0:T(8,128)(2,1)}, bf16[512,512]{1,0:T(8,128)(2,1)}, u32[]{:S(2)}, u32[]{:S(2)}) collective-permute-start(bf16[512,512]{1,0:T(8,128)(2,1)} %get-tuple-element.47), channel_id=1, source_target_pairs={{0,128},{128,0},{1,129},{129,1},{2,130},{130,2},{3,131},{131,3},{4... | collective-permute-start | bytes 1572872 | tf_op jit(solution)/shard_map/ppermute | solution.py:33
  56.7 26.6 %collective-permute-start.13 = (bf16[512,512]{1,0:T(8,128)(2,1)}, bf16[512,512]{1,0:T(8,128)(2,1)}, u32[]{:S(2)}, u32[]{:S(2)}) collective-permute-start(bf16[512,512]{1,0:T(8,128)(2,1)} %get-tuple-element.47), channel_id=1, source_target_pairs={{0,130},{2,128},{128,2},{130,0},{1,131},{3,129},{129,3},{131,1},{4... | collective-permute-start | bytes 1572872 | tf_op jit(solution)/shard_map/ppermute | solution.py:33
  60.7 16.5 %all-to-all-start.1 = ((bf16[4,64,2048]{2,1,0:T(8,128)(2,1)}), bf16[4,64,2048]{2,1,0:T(8,128)(2,1)S(1)}, u32[]{:S(2)}, u32[]{:S(2)}) async-start(bf16[4,64,2048]{2,1,0:T(8,128)(2,1)} %bitcast.80), calls=%async_computation.1 | async-start | bytes 2097152 | tf_op jit(solution)/shard_map/all_to_all | solution.py:67
  64.3 19.1 %collective-permute-start.12 = (bf16[512,512]{1,0:T(8,128)(2,1)}, bf16[512,512]{1,0:T(8,128)(2,1)}, u32[]{:S(2)}, u32[]{:S(2)}) collective-permute-start(bf16[512,512]{1,0:T(8,128)(2,1)} %get-tuple-element.46), channel_id=1, source_target_pairs={{0,128},{128,0},{1,129},{129,1},{2,130},{130,2},{3,131},{131,3},{4... | collective-permute-start | bytes 1572872 | tf_op jit(solution)/shard_map/ppermute | solution.py:33
  64.4 21.2 %collective-permute-start.14 = (bf16[512,512]{1,0:T(8,128)(2,1)}, bf16[512,512]{1,0:T(8,128)(2,1)}, u32[]{:S(2)}, u32[]{:S(2)}) collective-permute-start(bf16[512,512]{1,0:T(8,128)(2,1)} %get-tuple-element.46), channel_id=1, source_target_pairs={{0,130},{2,128},{128,2},{130,0},{1,131},{3,129},{129,3},{131,1},{4... | collective-permute-start | bytes 1572872 | tf_op jit(solution)/shard_map/ppermute | solution.py:33
  79.2 17.2 %all-to-all-start.2 = ((bf16[4,64,2048]{2,1,0:T(8,128)(2,1)}), bf16[4,64,2048]{2,1,0:T(8,128)(2,1)S(1)}, u32[]{:S(2)}, u32[]{:S(2)}) async-start(bf16[4,64,2048]{2,1,0:T(8,128)(2,1)} %copy-done.15), calls=%async_computation.2 | async-start | bytes 2097152 | tf_op jit(solution)/shard_map/all_to_all | solution.py:67
  108.5 73.3 %collective-permute-start.28 = (bf16[256,512]{1,0:T(8,128)(2,1)}, bf16[256,512]{1,0:T(8,128)(2,1)}, u32[]{:S(2)}, u32[]{:S(2)}) collective-permute-start(bf16[256,512]{1,0:T(8,128)(2,1)} %get-tuple-element.53), channel_id=1, source_target_pairs={{0,130},{2,128},{128,2},{130,0},{1,131},{3,129},{129,3},{131,1},{4... | collective-permute-start | bytes 786440 | tf_op jit(solution)/shard_map/ppermute | solution.py:33
  110.4 21.4 %collective-permute-start.20 = (bf16[2,128,512]{2,1,0:T(8,128)(2,1)}, bf16[2,128,512]{2,1,0:T(8,128)(2,1)S(1)}, u32[]{:S(2)}, u32[]{:S(2)}) collective-permute-start(bf16[2,128,512]{2,1,0:T(8,128)(2,1)} %get-tuple-element.28.own_ref), channel_id=1, source_target_pairs={{0,1},{1,0},{2,3},{3,2},{4,5},{5,4},{6,7},{7,6},{8,9},{9,8},{10,11... | collective-permute-start | bytes 786440 | tf_op jit(solution)/shard_map/ppermute | solution.py:33
  111.4 18.0 %all-to-all-start.3 = ((f32[32,4,128]{2,1,0:T(4,128)}), f32[32,4,128]{2,1,0:T(4,128)S(1)}, u32[]{:S(2)}, u32[]{:S(2)}) async-start(f32[32,4,128]{2,1,0:T(4,128)} %broadcast_in_dim.11), calls=%async_computation.3 | async-start | bytes 131072 | tf_op jit(solution)/shard_map/all_to_all | solution.py:67
  121.6 68.8 %collective-permute-start.34 = (bf16[256,1024]{1,0:T(8,128)(2,1)}, bf16[256,1024]{1,0:T(8,128)(2,1)}, u32[]{:S(2)}, u32[]{:S(2)}) collective-permute-start(bf16[256,1024]{1,0:T(8,128)(2,1)} %get-tuple-element.43), channel_id=1, source_target_pairs={{0,130},{2,128},{128,2},{130,0},{1,131},{3,129},{129,3},{131,1},{4... | collective-permute-start | bytes 1572872 | tf_op jit(solution)/shard_map/ppermute | solution.py:33
  139.2 15.6 %collective-permute-start.21 = (bf16[72,2048]{1,0:T(8,128)(2,1)S(1)}, bf16[72,2048]{1,0:T(8,128)(2,1)S(1)}, u32[]{:S(2)}, u32[]{:S(2)}) collective-permute-start(bf16[72,2048]{1,0:T(8,128)(2,1)S(1)} %get-tuple-element.31), channel_id=1, source_target_pairs={{0,32},{32,64},{64,96},{96,0},{1,33},{33,65},{65,97},{97,1},{2,34}... | collective-permute-start | bytes 884744 | tf_op jit(solution)/shard_map/ppermute | solution.py:33
  144.1 46.4 %collective-permute-start.33 = (bf16[256,1024]{1,0:T(8,128)(2,1)}, bf16[256,1024]{1,0:T(8,128)(2,1)}, u32[]{:S(2)}, u32[]{:S(2)}) collective-permute-start(bf16[256,1024]{1,0:T(8,128)(2,1)} %get-tuple-element.43), channel_id=1, source_target_pairs={{0,2},{2,0},{1,3},{3,1},{4,6},{6,4},{5,7},{7,5},{8,10},{10,8},{9,1... | collective-permute-start | bytes 1572872 | tf_op jit(solution)/shard_map/ppermute | solution.py:33
  146.3 48.1 %collective-permute-start.32 = (bf16[256,1024]{1,0:T(8,128)(2,1)}, bf16[256,1024]{1,0:T(8,128)(2,1)}, u32[]{:S(2)}, u32[]{:S(2)}) collective-permute-start(bf16[256,1024]{1,0:T(8,128)(2,1)} %get-tuple-element.42), channel_id=1, source_target_pairs={{0,128},{128,0},{1,129},{129,1},{2,130},{130,2},{3,131},{131,3},{4... | collective-permute-start | bytes 1572872 | tf_op jit(solution)/shard_map/ppermute | solution.py:33
  156.4 18.4 %all-to-all-start.4 = ((bf16[4,64,2048]{2,1,0:T(8,128)(2,1)}), bf16[4,64,2048]{2,1,0:T(8,128)(2,1)S(1)}, u32[]{:S(2)}, u32[]{:S(2)}) async-start(bf16[4,64,2048]{2,1,0:T(8,128)(2,1)} %broadcast_in_dim.12), calls=%async_computation.4 | async-start | bytes 2097152 | tf_op jit(solution)/shard_map/all_to_all | solution.py:67
  180.2 14.3 %collective-permute-start.37 = (bf16[256,512]{1,0:T(8,128)(2,1)S(1)}, bf16[256,512]{1,0:T(8,128)(2,1)S(1)}, u32[]{:S(2)}, u32[]{:S(2)}) collective-permute-start(bf16[256,512]{1,0:T(8,128)(2,1)S(1)} %copy-done.29), channel_id=1, source_target_pairs={{0,130},{2,128},{128,2},{130,0},{1,131},{3,129},{129,3},{131,1},{4... | collective-permute-start | bytes 786440 | tf_op jit(solution)/shard_map/ppermute | solution.py:33
  190.6 51.8 %collective-permute-start.31 = (bf16[256,1024]{1,0:T(8,128)(2,1)S(1)}, bf16[256,1024]{1,0:T(8,128)(2,1)S(1)}, u32[]{:S(2)}, u32[]{:S(2)}) collective-permute-start(bf16[256,1024]{1,0:T(8,128)(2,1)S(1)} %get-tuple-element.45), channel_id=1, source_target_pairs={{0,130},{2,128},{128,2},{130,0},{1,131},{3,129},{129,3},{131,1},{4... | collective-permute-start | bytes 1572872 | tf_op jit(solution)/shard_map/ppermute | solution.py:33
  194.4 48.0 %collective-permute-start.30 = (bf16[256,1024]{1,0:T(8,128)(2,1)S(1)}, bf16[256,1024]{1,0:T(8,128)(2,1)}, u32[]{:S(2)}, u32[]{:S(2)}) collective-permute-start(bf16[256,1024]{1,0:T(8,128)(2,1)S(1)} %get-tuple-element.45), channel_id=1, source_target_pairs={{0,2},{2,0},{1,3},{3,1},{4,6},{6,4},{5,7},{7,5},{8,10},{10,8},{9,1... | collective-permute-start | bytes 1572872 | tf_op jit(solution)/shard_map/ppermute | solution.py:33
  194.4 48.0 %collective-permute-start.29 = (bf16[256,1024]{1,0:T(8,128)(2,1)S(1)}, bf16[256,1024]{1,0:T(8,128)(2,1)}, u32[]{:S(2)}, u32[]{:S(2)}) collective-permute-start(bf16[256,1024]{1,0:T(8,128)(2,1)S(1)} %get-tuple-element.44), channel_id=1, source_target_pairs={{0,128},{128,0},{1,129},{129,1},{2,130},{130,2},{3,131},{131,3},{4... | collective-permute-start | bytes 1572872 | tf_op jit(solution)/shard_map/ppermute | solution.py:33
  195.8 14.5 %all-to-all-start.5 = ((bf16[8,128,128]{2,1,0:T(8,128)(2,1)}), bf16[8,128,128]{2,1,0:T(8,128)(2,1)S(1)}, u32[]{:S(2)}, u32[]{:S(2)}) async-start(bf16[8,128,128]{2,1,0:T(8,128)(2,1)} %bitcast.28), calls=%async_computation.5 | async-start | bytes 524288 | tf_op jit(solution)/shard_map/all_to_all | solution.py:67
  200.5 41.9 %collective-permute-start.26 = (bf16[256,512]{1,0:T(8,128)(2,1)}, bf16[256,512]{1,0:T(8,128)(2,1)}, u32[]{:S(2)}, u32[]{:S(2)}) collective-permute-start(bf16[256,512]{1,0:T(8,128)(2,1)} %get-tuple-element.53), channel_id=1, source_target_pairs={{0,128},{128,0},{1,129},{129,1},{2,130},{130,2},{3,131},{131,3},{4... | collective-permute-start | bytes 786440 | tf_op jit(solution)/shard_map/ppermute | solution.py:33
  201.7 32.5 %collective-permute-start.27 = (bf16[256,512]{1,0:T(8,128)(2,1)S(1)}, bf16[256,512]{1,0:T(8,128)(2,1)S(1)}, u32[]{:S(2)}, u32[]{:S(2)}) collective-permute-start(bf16[256,512]{1,0:T(8,128)(2,1)S(1)} %copy-done.27), channel_id=1, source_target_pairs={{0,2},{2,0},{1,3},{3,1},{4,6},{6,4},{5,7},{7,5},{8,10},{10,8},{9,1... | collective-permute-start | bytes 786440 | tf_op jit(solution)/shard_map/ppermute | solution.py:33
  (46 other events, 529.4 us)
